TPU v7x, 256 devices: a whole 4x4x8 slice. The times are simulated.
256 devices in a mesh: rows: 256 (over z, y, x, core).
Axes of the slice: x: 4, y: 4, z: 8, core: 2. Of those that a mesh axis runs over, the one named last changes fastest.
Arguments:
- trailing: float32 [131072, 1024], P('rows'), may hold values from -50 to 50
- leaf_vectors: float32 [131072, 256], P('rows'), may hold values from -2 to 2, as said below
- leaf_factors: float32 [65536, 256], P('rows'), may hold values from -2 to 2, as said below
- tree_vectors: float32 [65536, 256], P('rows'), may hold values from -2 to 2, as said below
- tree_factors: float32 [65536, 256], P('rows'), may hold values from -2 to 2, as said below
- inverse_factor: float32 [256, 256], replicated, may hold values from -2 to 2, as said below
Outputs:
- updated: float32 [131072, 1024], P('rows')
- panel_basis: float32 [131072, 256], P('rows')
- panel_gram: float32 [256, 256], replicated
Inputs may be any that keep to these rules, and one draw needn't show every extreme that they name: Within each leaf, rows 0 to 255 of leaf_vectors form a unit lower triangular matrix (ones on the diagonal, zeros above); leaf_factors_p is the upper triangular factor for which I - leaf_vectors_p leaf_factors_p leaf_vectors_p^T is orthogonal. `leaf_factors`: each block is upper triangular and is the factor described for leaf_vectors. `tree_vectors`: each block is upper triangular, diagonal included; with Y = [I; tree_vectors_q], I - Y tree_factors_q Y^T is orthogonal. `tree_factors`: each block is upper triangular and is the factor described for tree_vectors. `inverse_factor`: upper triangular with a positive diagonal.
All inputs are finite; a program needn't handle non-finite values.
Results may differ from a plain program's by a relative error of at most 0.00018.
Values sent between devices are 32-bit elements; how exact they have to be, the bound alone decides.
A program may use at most 64 MiB of HBM per device.

v0:
```python
import jax
import jax.numpy as jnp
from jax import lax
from jax.sharding import PartitionSpec as P

HIGHEST = lax.Precision.HIGHEST


def swapped(value, axis, stride):
    return lax.ppermute(value, axis, [(i, i ^ 1 << stride) for i in range(lax.axis_size(axis))])


def product(left_side, right_side):
    return jnp.dot(left_side, right_side, precision=HIGHEST, preferred_element_type=jnp.float32)


def across(left_side, right_side):
    return lax.dot_general(
        left_side,
        right_side,
        (((0,), (0,)), ((), ())),
        precision=HIGHEST,
        preferred_element_type=jnp.float32,
    )


def pair_update(lower_rows, upper_rows, vectors, factors):
    coeffs = across(factors, lower_rows + across(vectors, upper_rows))
    return (lower_rows - coeffs, upper_rows - product(vectors, coeffs))


def body(trailing, leaf_vectors, leaf_factors, tree_vectors, tree_factors, inverse_factor):
    panel_width = leaf_vectors.shape[1]
    devices = lax.axis_size("rows")
    levels = devices.bit_length() - 1
    my_index = lax.axis_index("rows")
    coeffs = across(leaf_factors, across(leaf_vectors, trailing))
    head_rows = trailing[:panel_width] - product(leaf_vectors[:panel_width], coeffs)
    rest_rows = trailing[panel_width:] - product(leaf_vectors[panel_width:], coeffs)
    rest_panel = rest_rows[:, :panel_width]
    for tree_level in range(levels):
        stride = 1 << tree_level
        position = my_index % (2 * stride)
        is_lower = position == 0
        is_upper = position == stride
        partner, partner_vectors, partner_factors = swapped(
            (head_rows, tree_vectors, tree_factors), "rows", tree_level
        )
        lower_rows = jnp.where(is_upper, partner, head_rows)
        upper_rows = jnp.where(is_upper, head_rows, partner)
        vectors = jnp.where(is_upper, tree_vectors, partner_vectors)
        factors = jnp.where(is_upper, tree_factors, partner_factors)
        low_new, high_new = pair_update(lower_rows, upper_rows, vectors, factors)
        head_rows = jnp.where(is_lower, low_new, jnp.where(is_upper, high_new, head_rows))
    is_first = my_index == 0
    head_panel = head_rows[:, :panel_width]
    head_gram = jnp.where(is_first, 0.0, across(head_panel, head_panel))
    gram_total = lax.psum(head_gram + across(rest_panel, rest_panel), "rows")
    total_rows = trailing.shape[0] * devices
    panel_gram = gram_total / float(total_rows)
    head_basis = jnp.where(is_first, 0.0, product(head_panel, inverse_factor))
    rest_basis = product(rest_panel, inverse_factor)
    panel_basis = jnp.concatenate([head_basis, rest_basis], axis=0)
    updated = jnp.concatenate([head_rows, rest_rows], axis=0)
    return (updated, panel_basis, panel_gram)


def solution(mesh):
    in_specs = (
        P("rows", None),
        P("rows", None),
        P("rows", None),
        P("rows", None),
        P("rows", None),
        P(),
    )
    out_specs = (P("rows", None), P("rows", None), P())
    return jax.shard_map(body, mesh=mesh, in_specs=in_specs, out_specs=out_specs, check_vma=False)
```

profile of v0, /device:TPU:17, one launch (start us, length us, event | category | flops | bytes accessed | tf_op | source)
XLA Modules:
  0.0 640.1 jit_solution(16034994768700524376)
XLA Ops:
  7.2 3.7 fusion.41
  15.2 2.3 collective-permute-done.2
  17.4 2.3 convolution_add_fusion.7
  20.9 3.5 subtract_select_fusion.7
  27.2 26.0 %collective-permute-done.5 = f32[256,256]{1,0:T(8,128)} collective-permute-done((f32[256,256]{1,0:T(8,128)S(1)}, f32[256,256]{1,0:T(8,128)}, u32[]{:S(2)}, u32[]{:S(2)}) %collective-permute-start.5) | collective-permute-done | bytes 262176 | tf_op jit(solution)/shard_map/ppermute | solution.py:10
  53.3 2.8 convolution_add_fusion.6
  56.1 2.8 collective-permute-done.4
  58.9 2.0 fusion.23
  60.9 2.9 subtract_select_fusion.6
  63.8 2.8 collective-permute-start.6
  66.9 2.7 collective-permute-start.7
  69.6 23.6 %collective-permute-done.8 = f32[256,256]{1,0:T(8,128)} collective-permute-done((f32[256,256]{1,0:T(8,128)S(1)}, f32[256,256]{1,0:T(8,128)}, u32[]{:S(2)}, u32[]{:S(2)}) %collective-permute-start.8) | collective-permute-done | bytes 262176 | tf_op jit(solution)/shard_map/ppermute | solution.py:10
  93.2 2.8 convolution_add_fusion.5
  96.0 2.8 collective-permute-done.7
  98.8 2.0 fusion.21
  100.8 3.6 subtract_select_fusion.5
  107.1 24.3 %collective-permute-done.11 = f32[256,256]{1,0:T(8,128)} collective-permute-done((f32[256,256]{1,0:T(8,128)S(1)}, f32[256,256]{1,0:T(8,128)}, u32[]{:S(2)}, u32[]{:S(2)}) %collective-permute-start.11) | collective-permute-done | bytes 262176 | tf_op jit(solution)/shard_map/ppermute | solution.py:10
  131.4 2.8 convolution_add_fusion.4
  134.3 2.9 collective-permute-done.10
  137.2 2.0 fusion.19
  139.2 2.9 subtract_select_fusion.4
  146.9 22.8 %collective-permute-done.14 = f32[256,256]{1,0:T(8,128)} collective-permute-done((f32[256,256]{1,0:T(8,128)S(1)}, f32[256,256]{1,0:T(8,128)}, u32[]{:S(2)}, u32[]{:S(2)}) %collective-permute-start.14) | collective-permute-done | bytes 262176 | tf_op jit(solution)/shard_map/ppermute | solution.py:10
  169.7 2.8 convolution_add_fusion.3
  172.5 2.8 collective-permute-done.13
  175.3 2.0 fusion.17
  177.3 3.6 subtract_select_fusion.3
  184.4 23.1 %collective-permute-done.17 = f32[256,256]{1,0:T(8,128)} collective-permute-done((f32[256,256]{1,0:T(8,128)S(1)}, f32[256,256]{1,0:T(8,128)}, u32[]{:S(2)}, u32[]{:S(2)}) %collective-permute-start.17) | collective-permute-done | bytes 262176 | tf_op jit(solution)/shard_map/ppermute | solution.py:10
  207.5 2.8 convolution_add_fusion.2
  210.3 2.9 collective-permute-done.16
  213.2 2.0 fusion.15
  215.2 2.9 subtract_select_fusion.2
  218.1 3.2 collective-permute-start.18
  221.4 2.3 collective-permute-start.19
  223.7 59.7 %collective-permute-done.20 = f32[256,256]{1,0:T(8,128)} collective-permute-done((f32[256,256]{1,0:T(8,128)S(1)}, f32[256,256]{1,0:T(8,128)}, u32[]{:S(2)}, u32[]{:S(2)}) %collective-permute-start.20) | collective-permute-done | bytes 262176 | tf_op jit(solution)/shard_map/ppermute | solution.py:10
  283.4 2.8 convolution_add_fusion.1
  286.2 2.8 collective-permute-done.19
  289.0 2.0 fusion.13
  291.0 3.1 subtract_select_fusion.1
  294.1 6.4 %collective-permute-start.21 = (f32[256,1024]{1,0:T(8,128)S(1)}, f32[256,1024]{1,0:T(8,128)}, u32[]{:S(2)}, u32[]{:S(2)}) collective-permute-start(f32[256,1024]{1,0:T(8,128)S(1)} %subtract_select_fusion.1), channel_id=1, source_target_pairs={{0,128},{1,129},{2,130},{3,131},{4,132},{5,133},{6,134},{7,135},{8... | collective-permute-start | bytes 3145736 | tf_op jit(solution)/shard_map/ppermute | solution.py:10
  300.6 5.4 collective-permute-start.22
  306.1 2.1 fusion.1
  309.6 53.3 %collective-permute-done.23 = f32[256,256]{1,0:T(8,128)} collective-permute-done((f32[256,256]{1,0:T(8,128)S(1)}, f32[256,256]{1,0:T(8,128)}, u32[]{:S(2)}, u32[]{:S(2)}) %collective-permute-start.23) | collective-permute-done | bytes 262176 | tf_op jit(solution)/shard_map/ppermute | solution.py:10
  362.9 2.7 convolution_add_fusion
  365.6 2.9 collective-permute-done.22
  368.5 2.0 fusion.11
  370.5 2.7 subtract_select_fusion
  375.9 2.8 pad_maximum_fusion
  379.5 251.9 %all-reduce.2.cloned.1.call-done = f32[256,256]{1,0:T(8,128)} async-done(((f32[256,256]{1,0:T(8,128)}), f32[256,256]{1,0:T(8,128)}) %all-reduce.2.cloned.1.call-update) | async-done | bytes 262160 | tf_op jit(solution)/shard_map/psum | solution.py:58
  (64 shorter events, 26.1 us)
Async XLA Ops:
  7.2 3.8 copy-start
  7.2 624.2 %all-reduce.2.cloned.1.call-start = ((), (), s32[]{:S(2)}) async-start(), calls=%async_computation | async-start | bytes 524288 | tf_op jit(solution)/shard_map/psum | solution.py:58
  7.2 5.5 copy-start.11
  10.9 1.8 copy-start.4
  12.8 1.9 copy-start.1
  12.8 2.0 copy-start.2
  13.9 3.6 collective-permute-start
  14.7 2.8 collective-permute-start.2
  14.8 5.0 collective-permute-start.1
  24.4 28.8 %collective-permute-start.3 = (f32[256,1024]{1,0:T(8,128)}, f32[256,1024]{1,0:T(8,128)S(1)}, u32[]{:S(2)}, u32[]{:S(2)}) collective-permute-start(f32[256,1024]{1,0:T(8,128)} %subtract_select_fusion.7), channel_id=1, source_target_pairs={{0,2},{1,3},{2,0},{3,1},{4,6},{5,7},{6,4},{7,5},{8,10},{9,11},{10,... | collective-permute-start | bytes 3145736 | tf_op jit(solution)/shard_map/ppermute | solution.py:10
  25.6 27.6 %collective-permute-start.5 = (f32[256,256]{1,0:T(8,128)S(1)}, f32[256,256]{1,0:T(8,128)}, u32[]{:S(2)}, u32[]{:S(2)}) collective-permute-start(f32[256,256]{1,0:T(8,128)S(1)} %copy-done.1), channel_id=1, source_target_pairs={{0,2},{1,3},{2,0},{3,1},{4,6},{5,7},{6,4},{7,5},{8,10},{9,11},{10,... | collective-permute-start | bytes 786440 | tf_op jit(solution)/shard_map/ppermute | solution.py:10
  25.9 33.0 %collective-permute-start.4 = (f32[256,256]{1,0:T(8,128)S(1)}, f32[256,256]{1,0:T(8,128)}, u32[]{:S(2)}, u32[]{:S(2)}) collective-permute-start(f32[256,256]{1,0:T(8,128)S(1)} %copy-done.2), channel_id=1, source_target_pairs={{0,2},{1,3},{2,0},{3,1},{4,6},{5,7},{6,4},{7,5},{8,10},{9,11},{10,... | collective-permute-start | bytes 786440 | tf_op jit(solution)/shard_map/ppermute | solution.py:10
  53.3 5.6 copy-start.8
  63.8 29.4 %collective-permute-start.6 = (f32[256,1024]{1,0:T(8,128)S(1)}, f32[256,1024]{1,0:T(8,128)}, u32[]{:S(2)}, u32[]{:S(2)}) collective-permute-start(f32[256,1024]{1,0:T(8,128)S(1)} %subtract_select_fusion.6), channel_id=1, source_target_pairs={{0,4},{1,5},{2,6},{3,7},{4,0},{5,1},{6,2},{7,3},{8,12},{9,13},{10,... | collective-permute-start | bytes 3145736 | tf_op jit(solution)/shard_map/ppermute | solution.py:10
  66.6 26.5 %collective-permute-start.8 = (f32[256,256]{1,0:T(8,128)S(1)}, f32[256,256]{1,0:T(8,128)}, u32[]{:S(2)}, u32[]{:S(2)}) collective-permute-start(f32[256,256]{1,0:T(8,128)S(1)} %copy-done.1), channel_id=1, source_target_pairs={{0,4},{1,5},{2,6},{3,7},{4,0},{5,1},{6,2},{7,3},{8,12},{9,13},{10,... | collective-permute-start | bytes 786440 | tf_op jit(solution)/shard_map/ppermute | solution.py:10
  66.9 31.9 %collective-permute-start.7 = (f32[256,256]{1,0:T(8,128)S(1)}, f32[256,256]{1,0:T(8,128)}, u32[]{:S(2)}, u32[]{:S(2)}) collective-permute-start(f32[256,256]{1,0:T(8,128)S(1)} %copy-done.2), channel_id=1, source_target_pairs={{0,4},{1,5},{2,6},{3,7},{4,0},{5,1},{6,2},{7,3},{8,12},{9,13},{10,... | collective-permute-start | bytes 786440 | tf_op jit(solution)/shard_map/ppermute | solution.py:10
  104.4 27.0 %collective-permute-start.9 = (f32[256,1024]{1,0:T(8,128)}, f32[256,1024]{1,0:T(8,128)S(1)}, u32[]{:S(2)}, u32[]{:S(2)}) collective-permute-start(f32[256,1024]{1,0:T(8,128)} %subtract_select_fusion.5), channel_id=1, source_target_pairs={{0,8},{1,9},{2,10},{3,11},{4,12},{5,13},{6,14},{7,15},{8,0},{9,1},... | collective-permute-start | bytes 3145736 | tf_op jit(solution)/shard_map/ppermute | solution.py:10
  105.4 26.0 %collective-permute-start.11 = (f32[256,256]{1,0:T(8,128)S(1)}, f32[256,256]{1,0:T(8,128)}, u32[]{:S(2)}, u32[]{:S(2)}) collective-permute-start(f32[256,256]{1,0:T(8,128)S(1)} %copy-done.1), channel_id=1, source_target_pairs={{0,8},{1,9},{2,10},{3,11},{4,12},{5,13},{6,14},{7,15},{8,0},{9,1},... | collective-permute-start | bytes 786440 | tf_op jit(solution)/shard_map/ppermute | solution.py:10
  105.9 31.3 %collective-permute-start.10 = (f32[256,256]{1,0:T(8,128)S(1)}, f32[256,256]{1,0:T(8,128)}, u32[]{:S(2)}, u32[]{:S(2)}) collective-permute-start(f32[256,256]{1,0:T(8,128)S(1)} %copy-done.2), channel_id=1, source_target_pairs={{0,8},{1,9},{2,10},{3,11},{4,12},{5,13},{6,14},{7,15},{8,0},{9,1},... | collective-permute-start | bytes 786440 | tf_op jit(solution)/shard_map/ppermute | solution.py:10
  131.4 5.7 copy-start.9
  142.1 27.6 %collective-permute-start.12 = (f32[256,1024]{1,0:T(8,128)S(1)}, f32[256,1024]{1,0:T(8,128)}, u32[]{:S(2)}, u32[]{:S(2)}) collective-permute-start(f32[256,1024]{1,0:T(8,128)S(1)} %subtract_select_fusion.4), channel_id=1, source_target_pairs={{0,16},{1,17},{2,18},{3,19},{4,20},{5,21},{6,22},{7,23},{8,24},{9,... | collective-permute-start | bytes 3145736 | tf_op jit(solution)/shard_map/ppermute | solution.py:10
  144.0 25.7 %collective-permute-start.14 = (f32[256,256]{1,0:T(8,128)S(1)}, f32[256,256]{1,0:T(8,128)}, u32[]{:S(2)}, u32[]{:S(2)}) collective-permute-start(f32[256,256]{1,0:T(8,128)S(1)} %copy-done.1), channel_id=1, source_target_pairs={{0,16},{1,17},{2,18},{3,19},{4,20},{5,21},{6,22},{7,23},{8,24},{9,... | collective-permute-start | bytes 786440 | tf_op jit(solution)/shard_map/ppermute | solution.py:10
  145.2 30.2 %collective-permute-start.13 = (f32[256,256]{1,0:T(8,128)S(1)}, f32[256,256]{1,0:T(8,128)}, u32[]{:S(2)}, u32[]{:S(2)}) collective-permute-start(f32[256,256]{1,0:T(8,128)S(1)} %copy-done.2), channel_id=1, source_target_pairs={{0,16},{1,17},{2,18},{3,19},{4,20},{5,21},{6,22},{7,23},{8,24},{9,... | collective-permute-start | bytes 786440 | tf_op jit(solution)/shard_map/ppermute | solution.py:10
  181.0 26.5 %collective-permute-start.15 = (f32[256,1024]{1,0:T(8,128)}, f32[256,1024]{1,0:T(8,128)S(1)}, u32[]{:S(2)}, u32[]{:S(2)}) collective-permute-start(f32[256,1024]{1,0:T(8,128)} %subtract_select_fusion.3), channel_id=1, source_target_pairs={{0,32},{1,33},{2,34},{3,35},{4,36},{5,37},{6,38},{7,39},{8,40},{9,... | collective-permute-start | bytes 3145736 | tf_op jit(solution)/shard_map/ppermute | solution.py:10
  182.5 24.9 %collective-permute-start.17 = (f32[256,256]{1,0:T(8,128)S(1)}, f32[256,256]{1,0:T(8,128)}, u32[]{:S(2)}, u32[]{:S(2)}) collective-permute-start(f32[256,256]{1,0:T(8,128)S(1)} %copy-done.1), channel_id=1, source_target_pairs={{0,32},{1,33},{2,34},{3,35},{4,36},{5,37},{6,38},{7,39},{8,40},{9,... | collective-permute-start | bytes 786440 | tf_op jit(solution)/shard_map/ppermute | solution.py:10
  182.5 30.6 %collective-permute-start.16 = (f32[256,256]{1,0:T(8,128)S(1)}, f32[256,256]{1,0:T(8,128)}, u32[]{:S(2)}, u32[]{:S(2)}) collective-permute-start(f32[256,256]{1,0:T(8,128)S(1)} %copy-done.2), channel_id=1, source_target_pairs={{0,32},{1,33},{2,34},{3,35},{4,36},{5,37},{6,38},{7,39},{8,40},{9,... | collective-permute-start | bytes 786440 | tf_op jit(solution)/shard_map/ppermute | solution.py:10
  207.5 5.7 copy-start.10
  218.1 70.9 %copy-start.3 = (f32[256,1024]{1,0:T(8,128)}, f32[256,1024]{1,0:T(8,128)S(1)}, u32[]{:S(2)}) copy-start(f32[256,1024]{1,0:T(8,128)S(1)} %subtract_select_fusion.2) | copy-start | bytes 3145732
  218.1 65.2 %collective-permute-start.18 = (f32[256,1024]{1,0:T(8,128)S(1)}, f32[256,1024]{1,0:T(8,128)}, u32[]{:S(2)}, u32[]{:S(2)}) collective-permute-start(f32[256,1024]{1,0:T(8,128)S(1)} %subtract_select_fusion.2), channel_id=1, source_target_pairs={{0,64},{1,65},{2,66},{3,67},{4,68},{5,69},{6,70},{7,71},{8,72},{9,... | collective-permute-start | bytes 3145736 | tf_op jit(solution)/shard_map/ppermute | solution.py:10
  221.3 62.1 %collective-permute-start.20 = (f32[256,256]{1,0:T(8,128)S(1)}, f32[256,256]{1,0:T(8,128)}, u32[]{:S(2)}, u32[]{:S(2)}) collective-permute-start(f32[256,256]{1,0:T(8,128)S(1)} %copy-done.1), channel_id=1, source_target_pairs={{0,64},{1,65},{2,66},{3,67},{4,68},{5,69},{6,70},{7,71},{8,72},{9,... | collective-permute-start | bytes 786440 | tf_op jit(solution)/shard_map/ppermute | solution.py:10
  221.4 67.6 %collective-permute-start.19 = (f32[256,256]{1,0:T(8,128)S(1)}, f32[256,256]{1,0:T(8,128)}, u32[]{:S(2)}, u32[]{:S(2)}) collective-permute-start(f32[256,256]{1,0:T(8,128)S(1)} %copy-done.2), channel_id=1, source_target_pairs={{0,64},{1,65},{2,66},{3,67},{4,68},{5,69},{6,70},{7,71},{8,72},{9,... | collective-permute-start | bytes 786440 | tf_op jit(solution)/shard_map/ppermute | solution.py:10
  291.0 15.0 %copy-start.5 = (f32[512,1024]{1,0:T(8,128)S(1)}, f32[512,1024]{1,0:T(8,128)}, u32[]{:S(2)}) copy-start(f32[512,1024]{1,0:T(8,128)} %param.6) | copy-start | bytes 6291460
  294.1 68.7 %collective-permute-start.21 = (f32[256,1024]{1,0:T(8,128)S(1)}, f32[256,1024]{1,0:T(8,128)}, u32[]{:S(2)}, u32[]{:S(2)}) collective-permute-start(f32[256,1024]{1,0:T(8,128)S(1)} %subtract_select_fusion.1), channel_id=1, source_target_pairs={{0,128},{1,129},{2,130},{3,131},{4,132},{5,133},{6,134},{7,135},{8... | collective-permute-start | bytes 3145736 | tf_op jit(solution)/shard_map/ppermute | solution.py:10
  300.5 62.3 %collective-permute-start.23 = (f32[256,256]{1,0:T(8,128)S(1)}, f32[256,256]{1,0:T(8,128)}, u32[]{:S(2)}, u32[]{:S(2)}) collective-permute-start(f32[256,256]{1,0:T(8,128)S(1)} %copy-done.1), channel_id=1, source_target_pairs={{0,128},{1,129},{2,130},{3,131},{4,132},{5,133},{6,134},{7,135},{8... | collective-permute-start | bytes 786440 | tf_op jit(solution)/shard_map/ppermute | solution.py:10
  300.6 67.8 %collective-permute-start.22 = (f32[256,256]{1,0:T(8,128)S(1)}, f32[256,256]{1,0:T(8,128)}, u32[]{:S(2)}, u32[]{:S(2)}) collective-permute-start(f32[256,256]{1,0:T(8,128)S(1)} %copy-done.2), channel_id=1, source_target_pairs={{0,128},{1,129},{2,130},{3,131},{4,132},{5,133},{6,134},{7,135},{8... | collective-permute-start | bytes 786440 | tf_op jit(solution)/shard_map/ppermute | solution.py:10
  370.5 3.7 copy-start.12
  370.5 4.1 copy-start.6
  373.2 1.0 copy-start.7
Sparse Core Ops, SparseCore 0:
  376.0 255.3 all-reduce.1
where the time goes:
time: 651 us; the launch traced here: 640 us
  waiting for transfers between devices  507 us (78%)
  matrix products  74.6 us (11%)
  starting transfers between devices  38.3 us (6%)
  between operations  14.6 us (2%)
    ppermute x24, waiting for transfers between devices, swapped(): lax.ppermute(value, axis, [(i, i ^ 1 << stride) for i in range(lax.axis_s...  255 us
    psum x1, waiting for transfers between devices, body(): gram_total = lax.psum(head_gram + across(rest_panel, rest_panel), 'rows')  252 us
    dot_general x20, matrix products, across(): lax.dot_general(left_side, right_side, (((0,), (0,)), ((), ())), precisio...  44.3 us
    ppermute x24, starting transfers between devices, swapped(): lax.ppermute(value, axis, [(i, i ^ 1 << stride) for i in range(lax.axis_s...  38.3 us
    dot_general x12, matrix products, product(): jnp.dot(left_side, right_side, precision=HIGHEST, preferred_element_type=...  30.3 us
  transfers between devices with their start and end apart: 25, of which 16 were waited for; matrix products, arithmetic and copies ran while one was open for 5% of the time, Pallas kernels for 0%

commit v1 on v0

v1 whole, which is shorter than its diff:
```python
import functools

import jax
import jax.numpy as jnp
from jax import lax
from jax.experimental import pallas as pl
from jax.experimental.pallas import tpu as pltpu
from jax.sharding import PartitionSpec as P

HIGH = lax.Precision.HIGH
F32 = jnp.float32
BF16 = jnp.bfloat16
ROW = 8
YDIM = 4


def product(left_side, right_side):
    return jnp.dot(left_side, right_side, precision=HIGH, preferred_element_type=F32)


def across(left_side, right_side):
    return lax.dot_general(
        left_side,
        right_side,
        (((0,), (0,)), ((), ())),
        precision=HIGH,
        preferred_element_type=F32,
    )


def halves(value):
    high = value.astype(BF16)
    low = (value - high.astype(F32)).astype(BF16)
    return high, low


def dot3(left_side, right_side, transposed=False):
    dims = (((1,), (1 if transposed else 0,)), ((), ()))
    left_high, left_low = halves(left_side)
    right_high, right_low = halves(right_side)

    def one(a, b):
        return lax.dot_general(a, b, dims, preferred_element_type=F32)

    return one(left_high, right_high) + (
        one(left_high, right_low) + one(left_low, right_high)
    )


def tree_kernel(
    devices,
    total_rows,
    head_ref,
    pack_ref,
    gram_ref,
    head_out,
    gram_out,
    ops,
    bop,
    cur0,
    cur1,
    cur2,
    z0, in0, w0, wb0,
    z1, in1, w1, wb1,
    z2, in2, w2, wb2,
    send3,
    recv3,
    back3,
    wback3,
    res1,
    res2,
    res3,
    gathered,
    gram_in,
    gram_piece,
    gram_level,
    panel,
    full,
    gram_all,
    send_sems,
    recv_sems,
):
    b = pack_ref.shape[1]
    nc = head_ref.shape[1]
    half, quarter, eighth = nc // 2, nc // 4, nc // 8
    rows = devices // ROW
    row_levels = rows.bit_length() - 1
    zdim = rows // YDIM
    piece = b // ROW
    me = lax.axis_index("rows")
    r = me % ROW
    g = me // ROW
    core = r % 2
    x0 = (r // 2) % 2
    x1 = r // 4
    base = g * ROW
    neighbour = base + (r + 1) % ROW
    y = g % YDIM
    first_y = y == 0

    def is_low(k):
        return g % (2 << k) == 0

    def is_member(other):
        return r == other

    def is_high(k):
        return g % (2 << k) == (1 << k)

    slot = [ops.at[i] for i in range(4 + row_levels)]
    wback = [wback3.at[k] for k in range(row_levels)]

    barrier = pltpu.get_barrier_semaphore()

    def meet(condition, other):
        @pl.when(condition)
        def _():
            pl.semaphore_signal(
                barrier, inc=1, device_id=(other,),
                device_id_type=pl.DeviceIdType.MESH,
            )

        return condition

    met = []
    for j in range(1, ROW):
        pl.semaphore_signal(
            barrier, inc=1, device_id=(base + (r + j) % ROW,),
            device_id_type=pl.DeviceIdType.MESH,
        )
    for k in range(row_levels):
        met.append(meet(is_low(k), me + (ROW << k)))
        met.append(meet(is_high(k), me - (ROW << k)))
    for z in range(1, zdim):
        if z & (z - 1):
            met.append(meet(g == 0, me + z * YDIM * ROW))
            met.append(meet(g == z * YDIM, me - z * YDIM * ROW))
    met.append(meet(first_y, me + 3 * ROW))
    met.append(meet(y == 3, me - 3 * ROW))
    peers = ROW - 1
    for condition in met:
        peers = peers + condition.astype(jnp.int32)
    pl.semaphore_wait(barrier, peers)

    counter = [0]
    pending = []

    def copy(source, target, number, other, condition=None):
        sem = counter[0]
        counter[0] += 1
        pltpu.make_async_remote_copy(
            src_ref=source,
            dst_ref=target,
            send_sem=send_sems.at[sem],
            recv_sem=recv_sems.at[number],
            device_id=(other,),
            device_id_type=pl.DeviceIdType.MESH,
        ).start()
        pending.append((condition, source, sem))

    def arrived(target, number):
        pltpu.make_async_remote_copy(
            src_ref=target,
            dst_ref=target,
            send_sem=send_sems.at[0],
            recv_sem=recv_sems.at[number],
            device_id=(neighbour,),
            device_id_type=pl.DeviceIdType.MESH,
        ).wait_recv()

    def when(condition, action):
        @pl.when(condition)
        def _():
            action()

    OPS, X0, W0, X1, W1, X2, W2, Z3, W3, GATHER, GROW, GLEV, PANEL, GZ, GY, GX = (
        0, 9, 10, 11, 12, 13, 14, 15, 20, 21, 29, 37, 42, 44, 45, 46,
    )

    row_id = lax.broadcasted_iota(jnp.int32, (b, b), 0)
    col_id = lax.broadcasted_iota(jnp.int32, (b, b), 1)

    def v_of(ref):
        return jnp.where(row_id <= col_id, ref[:b, :], 0.0)

    def a_of(ref):
        diagonal = jnp.where(row_id == col_id, ref[b : b + 1, :], 0.0)
        return jnp.where(row_id > col_id, ref[:b, :], diagonal)

    @pl.when(core == 1)
    def _():
        copy(pack_ref, slot[0], OPS + 0, me - 1, lambda: core == 1)
        ops[0] = pack_ref[...]

    @pl.when((r == 2) | (r == 6))
    def _():
        c = lambda: (r == 2) | (r == 6)
        copy(pack_ref, slot[1], OPS + 1, me - 2, c)
        copy(pack_ref, slot[1], OPS + 1, me + 1, c)
        ops[1] = pack_ref[...]

    @pl.when(r == 4)
    def _():
        for other in (0, 2, 6, 5):
            copy(pack_ref, slot[2], OPS + 2, base + other, lambda: r == 4)
        ops[2] = pack_ref[...]

    @pl.when(core == 0)
    def _():
        c = lambda: core == 0
        copy(head_ref.at[:, pl.ds(half, half)], in0, X0, me + 1, c)

    @pl.when(core == 1)
    def _():
        c = lambda: core == 1
        bop[0] = dot3(a_of(slot[0]), v_of(slot[0]), True)
        z0[...] = dot3(bop[0], head_ref[:, :half])
        copy(z0, in0, X0, me - 1, c)

    @pl.when(core == 0)
    def _():
        c = lambda: core == 0
        arrived(slot[0], OPS + 0)
        update = dot3(a_of(slot[0]), head_ref[:, :half])
        arrived(in0, X0)
        update = update + in0[...]
        cur0[...] = head_ref[:, :half] - update
        w0[...] = update

    @pl.when(core == 1)
    def _():
        arrived(in0, X0)
        update = dot3(a_of(slot[0]), in0[...]) + dot3(bop[0], head_ref[:, half:])
        cur0[...] = in0[...] - update
        w0[...] = update

    @pl.when(x0 == 0)
    def _():
        c = lambda: x0 == 0
        copy(cur0.at[:, pl.ds(quarter, quarter)], in1, X1, me + 2, c)

    @pl.when((r == 0) | (r == 4))
    def _():
        c = lambda: (r == 0) | (r == 4)
        arrived(slot[1], OPS + 1)
        copy(slot[1], slot[1], OPS + 1, me + 1, c)

    @pl.when((core == 1))
    def _():
        arrived(slot[1], OPS + 1)

    @pl.when(x0 == 1)
    def _():
        c = lambda: x0 == 1
        bop[1] = dot3(a_of(slot[1]), v_of(slot[1]), True)
        z1[...] = dot3(bop[1], cur0[:, :quarter])
        copy(z1, in1, X1, me - 2, c)

    @pl.when(core == 0)
    def _():
        c = lambda: core == 0
        copy(w0, wb0, W0, me + 1, c)

    for j in range(1, ROW):
        other = (r + j) % ROW
        copy(
            gram_ref.at[pl.ds(pl.multiple_of(other * piece, 8), piece), :],
            gram_in.at[ROW - j],
            GROW + ROW - j,
            base + other,
        )

    @pl.when((r == 0) & (g > 0))
    def _():
        c = lambda: (r == 0) & (g > 0)
        for other in (4, 2, 6, 1):
            copy(pack_ref, slot[3], OPS + 3, base + other, c)
        ops[3] = pack_ref[...]

    @pl.when((r == 0) | (r == 2) | (r == 6))
    def _():
        c = lambda: (r == 0) | (r == 2) | (r == 6)
        arrived(slot[2], OPS + 2)
        copy(slot[2], slot[2], OPS + 2, me + 1, c)

    @pl.when(x0 == 0)
    def _():
        c = lambda: x0 == 0
        update = dot3(a_of(slot[1]), cur0[:, :quarter])
        arrived(in1, X1)
        update = update + in1[...]
        cur1[...] = cur0[:, :quarter] - update
        w1[...] = update

    @pl.when(x0 == 1)
    def _():
        arrived(in1, X1)
        update = dot3(a_of(slot[1]), in1[...]) + dot3(bop[1], cur0[:, quarter:])
        cur1[...] = in1[...] - update
        w1[...] = update

    @pl.when(x1 == 0)
    def _():
        c = lambda: x1 == 0
        copy(cur1.at[:, pl.ds(eighth, eighth)], in2, X2, me + 4, c)

    @pl.when(core == 1)
    def _():
        arrived(slot[2], OPS + 2)

    @pl.when(x1 == 1)
    def _():
        c = lambda: x1 == 1
        bop[2] = dot3(a_of(slot[2]), v_of(slot[2]), True)
        z2[...] = dot3(bop[2], cur1[:, :eighth])
        copy(z2, in2, X2, me - 4, c)

    @pl.when(x0 == 0)
    def _():
        c = lambda: x0 == 0
        copy(w1, wb1, W1, me + 2, c)

    @pl.when((g > 0) & (core == 0))
    def _():
        c = lambda: (g > 0) & (core == 0) & (r > 0)

        @pl.when(r > 0)
        def _():
            arrived(slot[3], OPS + 3)
            copy(slot[3], slot[3], OPS + 3, me + 1, c)

    @pl.when((g > 0) & (core == 1))
    def _():
        arrived(slot[3], OPS + 3)

    for k in range(row_levels):
        @pl.when(is_high(k))
        def _():
            copy(slot[3], slot[4 + k], OPS + 4 + k, me - (ROW << k), functools.partial(is_high, k))

    @pl.when(core == 1)
    def _():
        v = v_of(slot[0])
        gathered[:, half:] = head_ref[:, half:] - dot3(v, w0[...])
        arrived(wb0, W0)
        gathered[:, :half] = head_ref[:, :half] - dot3(v, wb0[...])

    @pl.when(x1 == 0)
    def _():
        update = dot3(a_of(slot[2]), cur1[:, :eighth])
        arrived(in2, X2)
        update = update + in2[...]
        cur2[...] = cur1[:, :eighth] - update
        w2[...] = update

    @pl.when(x1 == 1)
    def _():
        arrived(in2, X2)
        update = dot3(a_of(slot[2]), in2[...]) + dot3(bop[2], cur1[:, eighth:])
        cur2[...] = in2[...] - update
        w2[...] = update

    for j in range(1, ROW):
        arrived(gram_in.at[ROW - j], GROW + ROW - j)
    own = gram_ref[pl.ds(pl.multiple_of(r * piece, 8), piece), :]
    for j in range(1, ROW):
        own = own + gram_in[j]
    gram_piece[...] = own

    @pl.when(g > 0)
    def _():
        bop[3] = dot3(a_of(slot[3]), v_of(slot[3]), True)

    for k in range(row_levels):
        @pl.when(is_high(k))
        def _():
            c = functools.partial(is_high, k)
            send3[...] = dot3(bop[3], cur2[...])
            copy(send3, recv3.at[k], Z3 + k, me - (ROW << k), c)
            copy(gram_piece, gram_level.at[k], GLEV + k, me - (ROW << k), c)

        if k == 0:
            @pl.when(x1 == 0)
            def _():
                c = lambda: x1 == 0
                copy(w2, wb2, W2, me + 4, c)

            @pl.when(x0 == 1)
            def _():
                v = v_of(slot[1])
                res1[:, quarter:] = cur0[:, quarter:] - dot3(v, w1[...])
                arrived(wb1, W1)
                res1[:, :quarter] = cur0[:, :quarter] - dot3(v, wb1[...])

            @pl.when((x0 == 1) & (core == 1))
            def _():
                c = lambda: (x0 == 1) & (core == 1)
                copy(res1, gathered.at[:, pl.ds(half, half)], GATHER + 1, me - 1, c)

            @pl.when((x0 == 1) & (core == 0))
            def _():
                gathered[:, :half] = res1[...]

        @pl.when(is_low(k))
        def _():
            c = functools.partial(is_low, k)
            arrived(slot[4 + k], OPS + 4 + k)
            update = dot3(a_of(slot[4 + k]), cur2[...])
            arrived(recv3.at[k], Z3 + k)
            update = update + recv3[k]
            cur2[...] = cur2[...] - update
            wback3[k] = update
            copy(wback[k], back3, W3, me + (ROW << k), c)
            arrived(gram_level.at[k], GLEV + k)
            gram_piece[...] = gram_piece[...] + gram_level[k]

        if k == 0:
            @pl.when(x1 == 1)
            def _():
                v = v_of(slot[2])
                res2[:, eighth:] = cur1[:, eighth:] - dot3(v, w2[...])
                arrived(wb2, W2)
                res2[:, :eighth] = cur1[:, :eighth] - dot3(v, wb2[...])

            for other, at in ((5, half), (6, quarter), (7, half + quarter)):
                @pl.when(r == other)
                def _():
                    copy(
                        res2, gathered.at[:, pl.ds(at, quarter)],
                        GATHER + other, base + 4, functools.partial(is_member, other),
                    )

            @pl.when(r == 4)
            def _():
                gathered[:, :quarter] = res2[...]

    for source, at in ((0, 0), (4, eighth)):
        @pl.when((g == 0) & (r == source))
        def _():
            c = functools.partial(lambda s: (g == 0) & (r == s), source)
            for j in range(1, ROW):
                copy(
                    cur2, panel.at[:, pl.ds(at, eighth)],
                    PANEL + source // 4, base + (r + j) % ROW, c,
                )
            panel[:, at : at + eighth] = cur2[...]

    @pl.when(g > 0)
    def _():
        arrived(back3, W3)
        res3[...] = cur2[...] - dot3(v_of(slot[3]), back3[...])

    @pl.when(g == 0)
    def _():
        res3[...] = cur2[...]

    for other in range(1, ROW):
        at = (other % 2) * half + (other // 2 % 2) * quarter + other // 4 * eighth

        @pl.when(r == other)
        def _():
            copy(
                res3, gathered.at[:, pl.ds(at, eighth)],
                GATHER + other, base, functools.partial(is_member, other),
            )

    @pl.when(r == 0)
    def _():
        gathered[:, :eighth] = res3[...]

    mine = pl.ds(pl.multiple_of(r * piece, 8), piece)

    @pl.when(g == 0)
    def _():
        @pl.when(r != 0)
        def _():
            arrived(panel.at[:, pl.ds(0, eighth)], PANEL)

        @pl.when(r != 4)
        def _():
            arrived(panel.at[:, pl.ds(eighth, eighth)], PANEL + 1)

        turned = panel[...].T
        full[...] = dot3(turned, turned, True)
        gram_all[mine, :] = (gram_piece[...] - full[mine, :]) / float(total_rows)
        for z in range(1, zdim):
            copy(
                gram_all.at[mine, :], gram_all.at[mine, :],
                GZ, me + z * YDIM * ROW, lambda: g == 0,
            )

    @pl.when(first_y)
    def _():
        @pl.when(g > 0)
        def _():
            arrived(gram_all.at[mine, :], GZ)

        for step in range(1, YDIM):
            copy(
                gram_all.at[mine, :], gram_all.at[mine, :],
                GY, me + step * ROW, lambda: y == 0,
            )

    @pl.when(y != 0)
    def _():
        arrived(gram_all.at[mine, :], GY)

    for j in range(1, ROW):
        copy(
            gram_all.at[mine, :], gram_all.at[mine, :],
            GX + ROW - j, base + (r + j) % ROW,
        )

    @pl.when((x0 == 1) & (core == 0))
    def _():
        arrived(gathered.at[:, pl.ds(half, half)], GATHER + 1)

    @pl.when(r == 4)
    def _():
        for other, at in ((5, half), (6, quarter), (7, half + quarter)):
            arrived(gathered.at[:, pl.ds(at, quarter)], GATHER + other)

    @pl.when(r == 0)
    def _():
        for other in range(1, ROW):
            at = (other % 2) * half + (other // 2 % 2) * quarter + other // 4 * eighth
            arrived(gathered.at[:, pl.ds(at, eighth)], GATHER + other)

    head_out[...] = gathered[...]
    for j in range(1, ROW):
        rows_j = pl.ds(pl.multiple_of((r + j) % ROW * piece, 8), piece)
        arrived(gram_all.at[rows_j, :], GX + j)
    gram_out[...] = gram_all[...]

    def sent(source, sem):
        pltpu.make_async_remote_copy(
            src_ref=source,
            dst_ref=source,
            send_sem=send_sems.at[sem],
            recv_sem=recv_sems.at[0],
            device_id=(neighbour,),
            device_id_type=pl.DeviceIdType.MESH,
        ).wait_send()

    for condition, source, sem in pending:
        if condition is None:
            sent(source, sem)
        else:
            when(condition(), functools.partial(sent, source, sem))


def tree(head, pack, gram, devices, total_rows):
    b, nc = pack.shape[1], head.shape[1]
    half, quarter, eighth = nc // 2, nc // 4, nc // 8
    piece = b // ROW
    levels = (devices // ROW).bit_length() - 1
    vmem = lambda *shape: pltpu.VMEM(shape, F32)
    whole = pl.BlockSpec(memory_space=pltpu.VMEM)
    scratch = [vmem(4 + levels, b + 8, b), vmem(4, b, b)]
    scratch += [vmem(b, half), vmem(b, quarter), vmem(b, eighth)]
    for width in (half, quarter, eighth):
        scratch += [vmem(b, width)] * 4
    scratch += [
        vmem(b, eighth),
        vmem(levels, b, eighth),
        vmem(b, eighth),
        vmem(levels, b, eighth),
        vmem(b, half),
        vmem(b, quarter),
        vmem(b, eighth),
        vmem(b, nc),
        vmem(ROW, piece, b),
        vmem(piece, b),
        vmem(levels, piece, b),
        vmem(b, b),
        vmem(b, b),
        vmem(b, b),
        pltpu.SemaphoreType.DMA((112,)),
        pltpu.SemaphoreType.DMA((64,)),
    ]
    return pl.pallas_call(
        functools.partial(tree_kernel, devices, total_rows),
        out_shape=(
            jax.ShapeDtypeStruct(head.shape, F32),
            jax.ShapeDtypeStruct((b, b), F32),
        ),
        in_specs=[whole] * 3,
        out_specs=(whole, whole),
        scratch_shapes=scratch,
        compiler_params=pltpu.CompilerParams(
            collective_id=0,
            has_side_effects=True,
            vmem_limit_bytes=48 * 1024 * 1024,
        ),
        name="tree",
    )(head, pack, gram)


def body(trailing, leaf_vectors, leaf_factors, tree_vectors, tree_factors, inverse_factor):
    b = leaf_vectors.shape[1]
    devices = lax.axis_size("rows")
    total_rows = trailing.shape[0] * devices
    coeffs = across(leaf_factors, across(leaf_vectors, trailing))
    head_rows = trailing[:b] - product(leaf_vectors[:b], coeffs)
    rest_rows = trailing[b:] - product(leaf_vectors[b:], coeffs)
    panel = trailing[:, :b]
    row_id = lax.broadcasted_iota(jnp.int32, (b, b), 0)
    col_id = lax.broadcasted_iota(jnp.int32, (b, b), 1)
    turned = tree_factors.T
    diagonal = jnp.sum(jnp.where(row_id == col_id, turned, 0.0), axis=0, keepdims=True)
    pack = jnp.concatenate(
        [
            jnp.where(row_id <= col_id, tree_vectors, turned),
            jnp.broadcast_to(diagonal, (8, b)),
        ],
        axis=0,
    )
    head_rows, panel_gram = tree(head_rows, pack, across(panel, panel), devices, total_rows)
    is_first = lax.axis_index("rows") == 0
    head_basis = jnp.where(is_first, 0.0, product(head_rows[:, :b], inverse_factor))
    rest_basis = product(rest_rows[:, :b], inverse_factor)
    panel_basis = jnp.concatenate([head_basis, rest_basis], axis=0)
    updated = jnp.concatenate([head_rows, rest_rows], axis=0)
    return (updated, panel_basis, panel_gram)


def solution(mesh):
    rows = P("rows", None)
    return jax.shard_map(
        body,
        mesh=mesh,
        in_specs=(rows, rows, rows, rows, rows, P()),
        out_specs=(rows, rows, P()),
        check_vma=False,
    )
```

time: 651 us -> 99 us (0.15)
  the two profiles are of different devices: /device:TPU:17 before, /device:TPU:53 now
where the time goes in v1:
time: 99 us; the launch traced here: 98.8 us
  Pallas kernels  84.2 us (85%)
  matrix products  7.23 us (7%)
  other arithmetic  3.53 us (4%)
  local copies, waits for them, and re-layouts  3.08 us (3%)
    pallas_call x1, Pallas kernels, tree(): pl.pallas_call(functools.partial(tree_kernel, devices, total_rows), out_s...  84.2 us
    dot_general x3, matrix products, across(): lax.dot_general(left_side, right_side, (((0,), (0,)), ((), ())), precisio...  4.5 us
    unnamed x12, local copies, waits for them, and re-layouts  3.07 us
    dot_general x4, matrix products, product(): jnp.dot(left_side, right_side, precision=HIGH, preferred_element_type=F32)  2.73 us

profile of v1, /device:TPU:53, one launch (start us, length us, event | category | flops | bytes accessed | tf_op | source)
XLA Modules:
  0.0 98.8 jit_solution(10104237652827422700)
XLA Ops:
  0.6 0.0 copy-start
  0.6 0.0 copy-start.3
  0.7 2.9 %fusion.10 = f32[256,1024]{1,0:T(8,128)S(1)} fusion(f32[512,256]{1,0:T(8,128)} %param.7, f32[512,1024]{1,0:T(8,128)} %param.6), kind=kOutput, calls=%fused_computation.20 | convolution fusion | flops 805306368 | bytes 3670016 | tf_op jit(solution)/shard_map/dot_general | solution.py:22
  3.6 0.0 copy-done
  3.6 0.0 copy-start.1
  3.6 1.0 %fusion.11 = f32[1024,256]{1,0:T(8,128)S(1)} fusion(f32[256,1024]{1,0:T(8,128)S(1)} %fusion.10, f32[256,256]{1,0:T(8,128)S(1)} %copy-done), kind=kOutput, calls=%fused_computation.21 | convolution fusion | flops 402653184 | bytes 2359296 | tf_op jit(solution)/shard_map/dot_general | solution.py:22
  4.6 0.0 copy-done.3
  4.6 0.6 copy-done.1
  5.2 1.6 %fusion.1 = f32[256,1024]{1,0:T(8,128)} fusion(f32[1024,256]{1,0:T(8,128)S(1)} %fusion.11, f32[512,1024]{1,0:T(8,128)S(1)} %copy-done.1, f32[512,256]{1,0:T(8,128)S(1)} %copy-done.3), kind=kOutput, calls=%fused_computation.4 | convolution fusion | flops 402915328 | bytes 3407872 | tf_op jit(solution)/shard_map/dot_general | solution.py:18
  6.7 0.6 fusion.head_ref
  7.4 1.8 %copy.10 = f32[256,256]{0,1:T(8,128)} copy(f32[256,256]{1,0:T(8,128)} %param.10) | data formatting | bytes 524288 | tf_op args[4]
  9.2 0.0 copy-start.2
  9.2 1.2 %bitcast_select_fusion.1 = (f32[256,256]{1,0:T(8,128)S(1)}, f32[256]{0:T(256)S(1)}) fusion(f32[256,256]{1,0:T(8,128)} %param.9, f32[256,256]{0,1:T(8,128)} %copy.10), kind=kLoop, calls=%fused_computation.13 | loop fusion | flops 327424 | bytes 787456 | tf_op jit(solution)/shard_map/jit(_where)/select_n | solution.py:613
  10.3 0.6 fusion.2.gram_ref
  11.0 84.2 %tree.1 = (f32[256,1024]{1,0:T(8,128)S(1)}, f32[256,256]{1,0:T(8,128)S(1)}) custom-call(f32[256,1024]{1,0:T(8,128)S(1)} %fusion.head_ref, f32[264,256]{1,0:T(8,128)S(1)} %pad_maximum_fusion.2.pack_ref, f32[256,256]{1,0:T(8,128)S(1)} %fusion.2.gram_ref), custom_call_target="tpu_custom_call" | custom-call | tf_op jit(solution)/shard_map/tree/pallas_call | solution.py:581
  95.2 0.0 copy-done.2
  95.2 0.0 copy-start.4
  95.2 1.5 %pad_maximum_fusion = f32[512,1024]{1,0:T(8,128)} fusion(f32[256,1024]{1,0:T(8,128)S(1)} %copy-done.2, f32[256,1024]{1,0:T(8,128)S(1)} %get-tuple-element.5), kind=kLoop, calls=%fused_computation | loop fusion | flops 524288 | bytes 4194304 | tf_op jit(solution)/shard_map/concatenate | solution.py:623
  96.7 0.0 copy-done.4
  96.7 0.3 fusion.4
  97.0 0.3 convolution_select_fusion
  97.3 0.8 pad_maximum_fusion.1
  98.1 0.7 copy.13
  (2 shorter events, 0.0 us)
Async XLA Ops:
  0.6 2.9 %copy-start = (f32[256,256]{1,0:T(8,128)S(1)}, f32[256,256]{1,0:T(8,128)}, u32[]{:S(2)}) copy-start(f32[256,256]{1,0:T(8,128)} %param.8) | copy-start | bytes 786436
  0.6 4.0 %copy-start.3 = (f32[512,256]{1,0:T(8,128)S(1)}, f32[512,256]{1,0:T(8,128)}, u32[]{:S(2)}) copy-start(f32[512,256]{1,0:T(8,128)} %param.7) | copy-start | bytes 1572868
  3.6 1.6 %copy-start.1 = (f32[512,1024]{1,0:T(8,128)S(1)}, f32[512,1024]{1,0:T(8,128)}, u32[]{:S(2)}) copy-start(f32[512,1024]{1,0:T(8,128)} %param.6) | copy-start | bytes 6291460
  9.2 86.0 %copy-start.2 = (f32[256,1024]{1,0:T(8,128)S(1)}, f32[256,1024]{1,0:T(8,128)}, u32[]{:S(2)}) copy-start(f32[256,1024]{1,0:T(8,128)} %fusion.1) | copy-start | bytes 3145732
  95.2 1.5 %copy-start.4 = (f32[256,256]{1,0:T(8,128)S(1)}, f32[256,256]{1,0:T(8,128)}, u32[]{:S(2)}) copy-start(f32[256,256]{1,0:T(8,128)} %param.11) | copy-start | bytes 786436

commit v2 on v0

v2 whole, which is shorter than its diff:
```python
import functools

import jax
import jax.numpy as jnp
from jax import lax
from jax.experimental import pallas as pl
from jax.experimental.pallas import tpu as pltpu
from jax.sharding import PartitionSpec as P

F32 = jnp.float32
BF16 = jnp.bfloat16
ROW = 8
YDIM = 4
MESH = pl.DeviceIdType.MESH


def halves(value):
    high = value.astype(BF16)
    low = (value - high.astype(F32)).astype(BF16)
    return high, low


def dot_pairs(left, right, transposed=False):
    dims = (((1,), (1 if transposed else 0,)), ((), ()))

    def one(a, b):
        return lax.dot_general(a, b, dims, preferred_element_type=F32)

    return one(left[0], right[0]) + (one(left[0], right[1]) + one(left[1], right[0]))


def dot3(left_side, right_side, transposed=False):
    return dot_pairs(halves(left_side), halves(right_side), transposed)


def tree_kernel(
    devices,
    total_rows,
    c_ref, lv_ref, lt_ref, tv_ref, tt_ref, inv_ref,
    upd_out, basis_out, gram_out,
    pack,
    ops,
    bt_high, bt_low,
    head,
    cur0, cur1, cur2,
    z0, z1, z2, in0, in1, in2, w0, w1, w2, wb0, wb1, wb2,
    zr, inr, wr, wbr,
    res1, res2, res3,
    gathered,
    coef, rest, rest_basis, head_rows, head_basis,
    lvt_high, lvt_low,
    gram_own, gram_in, gram_piece, gram_level, panel, gram_all,
    send_sems, recv_sems, local_sems,
):
    b = pack.shape[1]
    nc = c_ref.shape[1]
    row_count = devices // ROW
    row_levels = row_count.bit_length() - 1
    zdim = row_count // YDIM
    piece = b // ROW
    me = lax.axis_index("rows")
    r = me % ROW
    g = me // ROW
    core = r % 2
    x0 = (r // 2) % 2
    x1 = r // 4
    bits = (core, x0, x1)
    base = g * ROW
    y = g % YDIM
    neighbour = base + (r + 1) % ROW
    cur = (cur0, cur1, cur2)
    zs, ins, ws, wbs = (z0, z1, z2), (in0, in1, in2), (w0, w1, w2), (wb0, wb1, wb2)
    slot = [ops.at[i] for i in range(4 + row_levels)]
    CHUNKS = (0, 1)

    def slice_of(rank):
        return rank % 2 * 4 + rank // 2 % 2 * 2 + rank // 4

    def piece_of(rank):
        return pl.ds(pl.multiple_of(slice_of(rank) * piece, piece), piece)

    mine = piece_of(r)

    def size(level, chunk):
        return ((nc - b) // 2 if chunk else b // 2) >> level

    def own(level, chunk):
        return pl.ds((b // 2 >> level) if chunk else 0, size(level, chunk))

    def part(level, chunk, upper):
        start = (b >> level) if chunk else 0
        return pl.ds(start + (size(level, chunk) if upper else 0), size(level, chunk))

    def parent(level):
        return cur[level - 1] if level else head

    def is_low(k):
        return g % (2 << k) == 0

    def is_high(k):
        return g % (2 << k) == (1 << k)

    barrier = pltpu.get_barrier_semaphore()

    def greet(other):
        pl.semaphore_signal(barrier, inc=1, device_id=(other,), device_id_type=MESH)

    met = []

    def meet(condition, other):
        @pl.when(condition)
        def _():
            greet(other)

        met.append(condition)

    for j in range(1, ROW):
        greet(base + (r + j) % ROW)
    for k in range(row_levels):
        meet(is_low(k), me + (ROW << k))
        meet(is_high(k), me - (ROW << k))
    for z in range(1, zdim):
        if z & (z - 1):
            meet(g == 0, me + z * YDIM * ROW)
            meet(g == z * YDIM, me - z * YDIM * ROW)
    meet(y == 0, me + 3 * ROW)
    meet(y == 3, me - 3 * ROW)

    def entered():
        peers = ROW - 1
        for condition in met:
            peers = peers + condition.astype(jnp.int32)
        pl.semaphore_wait(barrier, peers)

    numbers = {}
    pending = []

    def number(*name):
        return numbers.setdefault(name, len(numbers))

    def remote(source, target, send, receive, other):
        return pltpu.make_async_remote_copy(
            src_ref=source,
            dst_ref=target,
            send_sem=send_sems.at[send],
            recv_sem=recv_sems.at[receive],
            device_id=(other,),
            device_id_type=MESH,
        )

    def copy(source, target, name, other, condition=None):
        remote(source, target, len(pending), number(*name), other).start()
        pending.append((condition, source))

    def arrived(target, name):
        remote(target, target, 0, number(*name), neighbour).wait_recv()

    row_id = lax.broadcasted_iota(jnp.int32, (b, b), 0)
    col_id = lax.broadcasted_iota(jnp.int32, (b, b), 1)

    def t_of(ref):
        return jnp.where(row_id <= col_id, ref[:b, :], 0.0)

    def vt_of(ref):
        diagonal = jnp.where(row_id == col_id, ref[b : b + 1, :], 0.0)
        return jnp.where(row_id > col_id, ref[:b, :], diagonal)

    def make_bt(index):
        high, low = halves(dot3(vt_of(slot[index]).T, t_of(slot[index])))
        bt_high[index] = high
        bt_low[index] = low

    def times_bt(value, index):
        return dot_pairs(halves(value), (bt_high[index], bt_low[index]))

    tv = tv_ref[...]
    pack[:b, :] = jnp.where(row_id <= col_id, tt_ref[...], tv.T)
    diagonal = jnp.sum(jnp.where(row_id == col_id, tv, 0.0), axis=0, keepdims=True)
    pack[b:, :] = jnp.broadcast_to(diagonal, (8, b))

    for condition, index in (
        (core == 1, 0), ((r == 2) | (r == 6), 1), (r == 4, 2), ((r == 0) & (g > 0), 3),
    ):
        @pl.when(condition)
        def _():
            ops[index] = pack[...]
            make_bt(index)

    high, low = halves(lv_ref[...].T)
    lvt_high[...] = high
    lvt_low[...] = low

    def leaf_tile(tile):
        columns = pl.ds(tile * b, b)
        inner = dot_pairs((lvt_high[...], lvt_low[...]), halves(c_ref[:, columns]))
        coeffs = dot3(lt_ref[...].T, inner)
        coef[:, columns] = coeffs
        result = c_ref[:b, columns] - dot3(lv_ref[:b, :], coeffs)
        head[columns, :] = result.T

    leaf_tile(0)
    entered()

    @pl.when(core == 1)
    def _():
        copy(pack, slot[0], ("ops", 0), me - 1, lambda: core == 1)

    @pl.when((r == 2) | (r == 6))
    def _():
        c = lambda: (r == 2) | (r == 6)
        copy(pack, slot[1], ("ops", 1), me + 1, c)
        copy(pack, slot[1], ("ops", 1), me - 2, c)

    @pl.when(r == 4)
    def _():
        for other in (5, 0, 2, 6):
            copy(pack, slot[2], ("ops", 2), base + other, lambda: r == 4)

    def send(level, chunk):
        bit, far = bits[level], 1 << level
        rows, name = own(level, chunk), ("x", level, chunk)
        target = ins[level].at[rows, :]
        low_rows, high_rows = part(level, chunk, False), part(level, chunk, True)

        @pl.when(bit == 0)
        def _():
            copy(
                parent(level).at[high_rows, :], target, name, me + far,
                lambda: bits[level] == 0,
            )

        source = zs[level].at[rows, :]

        @pl.when(bit == 1)
        def _():
            zs[level][rows, :] = times_bt(parent(level)[low_rows, :], level)
            copy(source, target, name, me - far, lambda: bits[level] == 1)

    def finish(level, chunk):
        bit = bits[level]
        rows, name = own(level, chunk), ("x", level, chunk)
        low_rows, high_rows = part(level, chunk, False), part(level, chunk, True)

        @pl.when(bit == 0)
        def _():
            value = parent(level)[low_rows, :]
            update = dot3(value, t_of(slot[level]))
            arrived(ins[level].at[rows, :], name)
            update = update + ins[level][rows, :]
            cur[level][rows, :] = value - update
            ws[level][rows, :] = update

        @pl.when(bit == 1)
        def _():
            update = times_bt(parent(level)[high_rows, :], level)
            arrived(ins[level].at[rows, :], name)
            value = ins[level][rows, :]
            update = update + dot3(value, t_of(slot[level]))
            cur[level][rows, :] = value - update
            ws[level][rows, :] = update

    def give_back(level, chunk):
        rows = own(level, chunk)

        @pl.when(bits[level] == 0)
        def _():
            copy(
                ws[level].at[rows, :], wbs[level].at[rows, :], ("w", level, chunk),
                me + (1 << level), lambda: bits[level] == 0,
            )

    def residual(level, result):
        @pl.when(bits[level] == 1)
        def _():
            vt = halves(vt_of(slot[level]))
            for chunk in CHUNKS:
                rows = own(level, chunk)
                low_rows, high_rows = part(level, chunk, False), part(level, chunk, True)
                result[high_rows, :] = parent(level)[high_rows, :] - dot_pairs(
                    halves(ws[level][rows, :]), vt
                )
                arrived(wbs[level].at[rows, :], ("w", level, chunk))
                result[low_rows, :] = parent(level)[low_rows, :] - dot_pairs(
                    halves(wbs[level][rows, :]), vt
                )

    def place(level, rank, chunk):
        shape = size(level - 1, chunk)
        start = b if chunk else 0
        for bit in range(level):
            start += (rank >> bit & 1) * size(bit, chunk)
        return pl.ds(start, shape)

    def buffer_rows(level, chunk):
        return pl.ds((b >> level) if chunk else 0, size(level - 1, chunk))

    def gather(level, result, rank, into):
        for chunk in CHUNKS:
            if rank == into:
                gathered[place(level, rank, chunk), :] = result[buffer_rows(level, chunk), :]
            else:
                copy(
                    result.at[buffer_rows(level, chunk), :],
                    gathered.at[place(level, rank, chunk), :],
                    ("gather", rank % 4 if level == 1 else rank, chunk),
                    base + into, lambda: r == rank,
                )

    def gather_wait(level, rank):
        for chunk in CHUNKS:
            arrived(
                gathered.at[place(level, rank, chunk), :],
                ("gather", rank % 4 if level == 1 else rank, chunk),
            )

    send(0, 0)
    for tile in range(1, nc // b):
        leaf_tile(tile)
    send(0, 1)

    @pl.when(core == 0)
    def _():
        arrived(slot[0], ("ops", 0))

    finish(0, 0)

    @pl.when((r == 3) | (r == 7))
    def _():
        arrived(slot[1], ("ops", 1))
        make_bt(1)

    send(1, 0)

    @pl.when((r == 0) & (g > 0))
    def _():
        for other in (1, 2, 6, 4):
            copy(pack, slot[3], ("ops", 3), base + other, lambda: (r == 0) & (g > 0))

    finish(0, 1)
    send(1, 1)

    @pl.when((r == 0) | (r == 4))
    def _():
        arrived(slot[1], ("ops", 1))
        copy(slot[1], slot[1], ("ops", 1), me + 1, lambda: (r == 0) | (r == 4))

    columns = c_ref[:, :b]
    gram_own[...] = dot3(columns.T, columns)
    for j in range(1, ROW):
        other = (r + j) % ROW
        copy(
            gram_own.at[piece_of(other), :], gram_in.at[ROW - j],
            ("gram", ROW - j), base + other,
        )
    give_back(0, 0)
    give_back(0, 1)

    @pl.when((r == 1) | (r == 5))
    def _():
        arrived(slot[1], ("ops", 1))

    @pl.when((r == 0) | (r == 2) | (r == 6))
    def _():
        arrived(slot[2], ("ops", 2))
        copy(slot[2], slot[2], ("ops", 2), me + 1, lambda: (r == 0) | (r == 2) | (r == 6))

    finish(1, 0)

    @pl.when(core == 1)
    def _():
        arrived(slot[2], ("ops", 2))

    @pl.when((x1 == 1) & (r > 4))
    def _():
        make_bt(2)

    send(2, 0)
    finish(1, 1)
    send(2, 1)
    give_back(1, 0)
    give_back(1, 1)

    @pl.when((g > 0) & (core == 0) & (r > 0))
    def _():
        arrived(slot[3], ("ops", 3))
        copy(
            slot[3], slot[3], ("ops", 3), me + 1,
            lambda: (g > 0) & (core == 0) & (r > 0),
        )

    for k in range(row_levels):
        @pl.when(is_high(k) & (core == 0))
        def _():
            copy(
                slot[3], slot[4 + k], ("ops", 4 + k), me - (ROW << k),
                functools.partial(lambda k: is_high(k) & (core == 0), k),
            )

    def rest_tile(tile):
        columns = pl.ds(tile * b, b)
        rest[:, columns] = c_ref[b:, columns] - dot3(lv_ref[b:, :], coef[:, columns])

    rest_tile(0)
    rest_basis[...] = dot3(rest[:, :b], inv_ref[...])
    for tile in range(1, nc // b):
        rest_tile(tile)
    local = [
        pltpu.make_async_copy(rest, upd_out.at[pl.ds(b, b), :], local_sems.at[0]),
        pltpu.make_async_copy(rest_basis, basis_out.at[pl.ds(b, b), :], local_sems.at[1]),
    ]
    for made in local:
        made.start()

    @pl.when((g > 0) & (core == 1))
    def _():
        arrived(slot[3], ("ops", 3))

    @pl.when((g > 0) & (r > 0))
    def _():
        make_bt(3)

    def send_row(k, chunk):
        rows = own(2, chunk)
        source = zr.at[rows, :]

        @pl.when(is_high(k))
        def _():
            zr[rows, :] = times_bt(cur2[rows, :], 3)
            copy(
                source, inr.at[k, rows, :], ("z", k, chunk), me - (ROW << k),
                functools.partial(is_high, k),
            )

    def finish_row(k, chunk):
        rows = own(2, chunk)
        source = wr.at[k, rows, :]

        @pl.when(is_low(k))
        def _():
            value = cur2[rows, :]
            update = dot3(value, t_of(slot[4 + k]))
            arrived(inr.at[k, rows, :], ("z", k, chunk))
            update = update + inr[k, rows, :]
            cur2[rows, :] = value - update
            wr[k, rows, :] = update
            copy(
                source, wbr.at[rows, :], ("wr", chunk), me + (ROW << k),
                functools.partial(is_low, k),
            )

    def row_operators(k):
        @pl.when(is_low(k) & (core == 0))
        def _():
            arrived(slot[4 + k], ("ops", 4 + k))
            copy(
                slot[4 + k], slot[4 + k], ("ops", 4 + k), me + 1,
                functools.partial(lambda k: is_low(k) & (core == 0), k),
            )

        @pl.when(is_low(k) & (core == 1))
        def _():
            arrived(slot[4 + k], ("ops", 4 + k))

    finish(2, 0)
    send_row(0, 0)
    finish(2, 1)
    send_row(0, 1)
    give_back(2, 0)
    give_back(2, 1)

    residual(0, gathered)

    for j in range(1, ROW):
        arrived(gram_in.at[ROW - j], ("gram", ROW - j))
    total = gram_own[mine, :]
    for j in range(1, ROW):
        total = total + gram_in[j]
    gram_piece[...] = total

    for k in range(row_levels):
        row_operators(k)
        finish_row(k, 0)
        if k + 1 < row_levels:
            send_row(k + 1, 0)
        else:
            @pl.when(g == 0)
            def _():
                panel[mine, :] = cur2[own(2, 0), :]
                for j in range(1, ROW):
                    copy(
                        cur2.at[own(2, 0), :], panel.at[mine, :],
                        ("panel", ROW - j), base + (r + j) % ROW, lambda: g == 0,
                    )

        finish_row(k, 1)
        if k + 1 < row_levels:
            send_row(k + 1, 1)

        @pl.when(is_high(k))
        def _():
            copy(
                gram_piece, gram_level.at[k], ("level", k), me - (ROW << k),
                functools.partial(is_high, k),
            )

        @pl.when(is_low(k))
        def _():
            arrived(gram_level.at[k], ("level", k))
            gram_piece[...] = gram_piece[...] + gram_level[k]

        if k == 0:
            residual(1, res1)
            for rank, into in ((2, 2), (3, 2), (6, 6), (7, 6)):
                @pl.when(r == rank)
                def _():
                    gather(1, res1, rank, into)
        if k == 1 or row_levels == 1:
            residual(2, res2)
            for rank in range(4, ROW):
                @pl.when(r == rank)
                def _():
                    gather(2, res2, rank, 4)

    @pl.when(g > 0)
    def _():
        vt = halves(vt_of(slot[3]))
        for chunk in CHUNKS:
            rows = own(2, chunk)
            arrived(wbr.at[rows, :], ("wr", chunk))
            res3[rows, :] = cur2[rows, :] - dot_pairs(halves(wbr[rows, :]), vt)

    @pl.when(g == 0)
    def _():
        res3[...] = cur2[...]

    for rank in range(ROW):
        @pl.when(r == rank)
        def _():
            gather(3, res3, rank, 0)

    @pl.when(g == 0)
    def _():
        for j in range(1, ROW):
            arrived(panel.at[piece_of((r + j) % ROW), :], ("panel", j))
        square = dot3(panel[mine, :], panel[...], True)
        gram_all[mine, :] = (gram_piece[...] - square) / float(total_rows)
        for z in range(1, zdim):
            copy(
                gram_all.at[mine, :], gram_all.at[mine, :], ("gz",),
                me + z * YDIM * ROW, lambda: g == 0,
            )

    @pl.when(y == 0)
    def _():
        @pl.when(g > 0)
        def _():
            arrived(gram_all.at[mine, :], ("gz",))

        for step in range(1, YDIM):
            copy(
                gram_all.at[mine, :], gram_all.at[mine, :], ("gy",),
                me + step * ROW, lambda: y == 0,
            )

    @pl.when(y != 0)
    def _():
        arrived(gram_all.at[mine, :], ("gy",))

    for j in range(1, ROW):
        copy(
            gram_all.at[mine, :], gram_all.at[mine, :], ("gx", ROW - j),
            base + (r + j) % ROW,
        )

    @pl.when((x0 == 1) & (core == 0))
    def _():
        gather_wait(1, 3)

    @pl.when(r == 4)
    def _():
        for rank in (5, 6, 7):
            gather_wait(2, rank)

    @pl.when(r == 0)
    def _():
        for rank in range(1, ROW):
            gather_wait(3, rank)

    head_rows[...] = gathered[...].T
    head_basis[...] = jnp.where(me == 0, 0.0, dot3(head_rows[:, :b], inv_ref[...]))
    local += [
        pltpu.make_async_copy(head_rows, upd_out.at[pl.ds(0, b), :], local_sems.at[2]),
        pltpu.make_async_copy(head_basis, basis_out.at[pl.ds(0, b), :], local_sems.at[3]),
    ]
    for made in local[2:]:
        made.start()
    for j in range(1, ROW):
        arrived(gram_all.at[piece_of((r + j) % ROW), :], ("gx", j))
    local.append(pltpu.make_async_copy(gram_all, gram_out, local_sems.at[4]))
    local[-1].start()

    for index, (condition, source) in enumerate(pending):
        made = functools.partial(
            lambda source, index: remote(source, source, index, 0, neighbour).wait_send(),
            source, index,
        )
        if condition is None:
            made()
        else:
            @pl.when(condition())
            def _():
                made()
    for made in local:
        made.wait()


def body(trailing, leaf_vectors, leaf_factors, tree_vectors, tree_factors, inverse_factor):
    b, nc = leaf_vectors.shape[1], trailing.shape[1]
    devices = lax.axis_size("rows")
    total_rows = trailing.shape[0] * devices
    levels = (devices // ROW).bit_length() - 1
    piece = b // ROW

    def vmem(*shape, dtype=F32):
        return pltpu.VMEM(shape, dtype)

    per_level = [vmem(nc >> level, b) for level in (1, 2, 3)]
    scratch = [
        vmem(b + 8, b),
        vmem(4 + levels, b + 8, b),
        vmem(4, b, b, dtype=BF16),
        vmem(4, b, b, dtype=BF16),
        vmem(nc, b),
        *per_level,
        *per_level, *per_level, *per_level, *per_level,
        vmem(nc // 8, b), vmem(levels, nc // 8, b), vmem(levels, nc // 8, b),
        vmem(nc // 8, b),
        *per_level,
        vmem(nc, b),
        vmem(b, nc), vmem(b, nc), vmem(b, b), vmem(b, nc), vmem(b, b),
        vmem(b, 2 * b, dtype=BF16), vmem(b, 2 * b, dtype=BF16),
        vmem(b, b), vmem(ROW, piece, b), vmem(piece, b), vmem(levels, piece, b),
        vmem(b, b), vmem(b, b),
        pltpu.SemaphoreType.DMA((200,)),
        pltpu.SemaphoreType.DMA((96,)),
        pltpu.SemaphoreType.DMA((5,)),
    ]
    return pl.pallas_call(
        functools.partial(tree_kernel, devices, total_rows),
        out_shape=(
            jax.ShapeDtypeStruct(trailing.shape, F32),
            jax.ShapeDtypeStruct(leaf_vectors.shape, F32),
            jax.ShapeDtypeStruct((b, b), F32),
        ),
        in_specs=[pl.BlockSpec(memory_space=pltpu.VMEM)] * 6,
        out_specs=[pl.BlockSpec(memory_space=pl.ANY)] * 3,
        scratch_shapes=scratch,
        compiler_params=pltpu.CompilerParams(
            collective_id=0,
            has_side_effects=True,
            vmem_limit_bytes=48 * 1024 * 1024,
        ),
        name="tree",
    )(trailing, leaf_vectors, leaf_factors, tree_vectors, tree_factors, inverse_factor)


def solution(mesh):
    rows = P("rows", None)
    return jax.shard_map(
        body,
        mesh=mesh,
        in_specs=(rows, rows, rows, rows, rows, P()),
        out_specs=(rows, rows, P()),
        check_vma=False,
    )
```

time: 651 us -> 87.6 us (0.13)
  the two profiles are of different devices: /device:TPU:17 before, /device:TPU:49 now
where the time goes in v2:
time: 87.6 us; the launch traced here: 87.4 us
  Pallas kernels  79 us (90%)
  local copies, waits for them, and re-layouts  7.65 us (9%)
    pallas_call x1, Pallas kernels, body(): pl.pallas_call(functools.partial(tree_kernel, devices, total_rows), out_s...  79 us
    unnamed x13, local copies, waits for them, and re-layouts  7.65 us

profile of v2, /device:TPU:49, one launch (start us, length us, event | category | flops | bytes accessed | tf_op | source)
XLA Modules:
  0.0 87.4 jit_solution(8012070770793421325)
XLA Ops:
  0.6 0.0 copy-start
  0.6 1.0 %copy-done = f32[512,256]{1,0:T(8,128)S(1)} copy-done((f32[512,256]{1,0:T(8,128)S(1)}, f32[512,256]{1,0:T(8,128)}, u32[]{:S(2)}) %copy-start) | copy-done | bytes 524312
  1.7 0.0 copy-start.1
  1.7 0.9 %copy-done.1 = f32[256,256]{1,0:T(8,128)S(1)} copy-done((f32[256,256]{1,0:T(8,128)S(1)}, f32[256,256]{1,0:T(8,128)}, u32[]{:S(2)}) %copy-start.1) | copy-done | bytes 262168
  2.6 0.0 copy-start.2
  2.6 0.9 %copy-done.2 = f32[256,256]{1,0:T(8,128)S(1)} copy-done((f32[256,256]{1,0:T(8,128)S(1)}, f32[256,256]{1,0:T(8,128)}, u32[]{:S(2)}) %copy-start.2) | copy-done | bytes 262168
  3.6 0.0 copy-start.3
  3.6 0.9 %copy-done.3 = f32[256,256]{1,0:T(8,128)S(1)} copy-done((f32[256,256]{1,0:T(8,128)S(1)}, f32[256,256]{1,0:T(8,128)}, u32[]{:S(2)}) %copy-start.3) | copy-done | bytes 262168
  4.5 0.0 copy-start.4
  4.5 0.9 %copy-done.4 = f32[256,256]{1,0:T(8,128)S(1)} copy-done((f32[256,256]{1,0:T(8,128)S(1)}, f32[256,256]{1,0:T(8,128)}, u32[]{:S(2)}) %copy-start.4) | copy-done | bytes 262168
  5.5 79.0 %tree.1 = (f32[512,1024]{1,0:T(8,128)S(1)}, f32[512,256]{1,0:T(8,128)S(1)}, f32[256,256]{1,0:T(8,128)S(1)}) custom-call(f32[512,1024]{1,0:T(8,128)} %c_ref.1, f32[512,256]{1,0:T(8,128)S(1)} %copy-done, f32[256,256]{1,0:T(8,128)S(1)} %copy-done.1, f32[256,256]{1,0:T(8,128)S(1)} %copy-done.2, f32[256,256]{1,0:T(8,128)S(1)} %copy-done.3, f32[256,256]{1,0:T(8,128)S(1)} %copy-done.4), custom_call_target="tpu_custom_call" | custom-call | tf_op jit(solution)/shard_map/tree/pallas_call | solution.py:648
  84.5 1.3 %copy.12 = f32[512,1024]{1,0:T(8,128)} copy(f32[512,1024]{1,0:T(8,128)S(1)} %get-tuple-element.6) | data formatting | bytes 4194304
  85.9 0.8 copy.13
  86.6 0.7 copy.14
Async XLA Ops:
  0.6 1.0 %copy-start = (f32[512,256]{1,0:T(8,128)S(1)}, f32[512,256]{1,0:T(8,128)}, u32[]{:S(2)}) copy-start(f32[512,256]{1,0:T(8,128)} %lv_ref.1) | copy-start | bytes 1572868
  1.7 0.9 %copy-start.1 = (f32[256,256]{1,0:T(8,128)S(1)}, f32[256,256]{1,0:T(8,128)}, u32[]{:S(2)}) copy-start(f32[256,256]{1,0:T(8,128)} %lt_ref.1) | copy-start | bytes 786436
  2.6 0.9 %copy-start.2 = (f32[256,256]{1,0:T(8,128)S(1)}, f32[256,256]{1,0:T(8,128)}, u32[]{:S(2)}) copy-start(f32[256,256]{1,0:T(8,128)} %tv_ref.1) | copy-start | bytes 786436
  3.6 0.9 %copy-start.3 = (f32[256,256]{1,0:T(8,128)S(1)}, f32[256,256]{1,0:T(8,128)}, u32[]{:S(2)}) copy-start(f32[256,256]{1,0:T(8,128)} %tt_ref.1) | copy-start | bytes 786436
  4.5 0.9 %copy-start.4 = (f32[256,256]{1,0:T(8,128)S(1)}, f32[256,256]{1,0:T(8,128)}, u32[]{:S(2)}) copy-start(f32[256,256]{1,0:T(8,128)} %inv_ref.1) | copy-start | bytes 786436

commit v3 on v2

v3 whole, which is shorter than its diff:
```python
import functools

import jax
import jax.numpy as jnp
from jax import lax
from jax.experimental import pallas as pl
from jax.experimental.pallas import tpu as pltpu
from jax.sharding import PartitionSpec as P

F32 = jnp.float32
BF16 = jnp.bfloat16
ROW = 8
YDIM = 4
MESH = pl.DeviceIdType.MESH
RECEIVES = 56


def halves(value):
    high = value.astype(BF16)
    low = (value - high.astype(F32)).astype(BF16)
    return high, low


def dot_pairs(left, right, transposed=False):
    dims = (((1,), (1 if transposed else 0,)), ((), ()))

    def one(a, b):
        return lax.dot_general(a, b, dims, preferred_element_type=F32)

    return one(left[0], right[0]) + (one(left[0], right[1]) + one(left[1], right[0]))


def dot3(left_side, right_side, transposed=False):
    return dot_pairs(halves(left_side), halves(right_side), transposed)


def tree_kernel(
    devices,
    total_rows,
    c_hbm, lv_hbm, lt_hbm, tv_hbm, tt_hbm, inv_hbm,
    upd_out, basis_out, gram_out,
    c_ref, lv_ref, lt_ref, tv_ref, tt_ref, inv_ref,
    pack,
    folded,
    slot0, slot1, slot2, slot3,
    fold,
    row_fold,
    t_high, t_low,
    bt_high, bt_low,
    head,
    cur0, cur1, cur2,
    z0, z1, z2, in0, in1, in2, w0, w1, w2, wb0, wb1, wb2,
    zr, inr, wr, wbr,
    res1, res2, res3,
    gathered,
    coef, rest, rest_basis, head_rows, head_basis,
    lvt_high, lvt_low,
    gram_own, gram_in, gram_piece, gram_level, panel, gram_all,
    send_sem, recv_sems, local_sems,
):
    b = pack.shape[1]
    hb = b // 2
    nc = c_ref.shape[1]
    row_count = devices // ROW
    row_levels = row_count.bit_length() - 1
    zdim = row_count // YDIM
    piece = b // ROW
    me = lax.axis_index("rows")
    r = me % ROW
    g = me // ROW
    core = r % 2
    x0 = (r // 2) % 2
    x1 = r // 4
    bits = (core, x0, x1)
    base = g * ROW
    y = g % YDIM
    neighbour = base + (r + 1) % ROW
    cur = (cur0, cur1, cur2)
    zs, ins, ws, wbs = (z0, z1, z2), (in0, in1, in2), (w0, w1, w2), (wb0, wb1, wb2)
    slot = (slot0, slot1, slot2, slot3)
    folds = [fold.at[i] for i in range(3 + row_levels)]
    CHUNKS = (0, 1)
    eighth_b = (nc - b) // 8
    ROW_CHUNKS = (
        pl.ds(0, piece),
        pl.ds(piece, eighth_b // 2),
        pl.ds(piece + eighth_b // 2, eighth_b // 2),
    )

    def slice_of(rank):
        return rank % 2 * 4 + rank // 2 % 2 * 2 + rank // 4

    def piece_of(rank):
        return pl.ds(pl.multiple_of(slice_of(rank) * piece, piece), piece)

    mine = piece_of(r)

    def size(level, chunk):
        return ((nc - b) // 2 if chunk else b // 2) >> level

    def own(level, chunk):
        return pl.ds((b // 2 >> level) if chunk else 0, size(level, chunk))

    def part(level, chunk, upper):
        start = (b >> level) if chunk else 0
        return pl.ds(start + (size(level, chunk) if upper else 0), size(level, chunk))

    def parent(level):
        return cur[level - 1] if level else head

    def is_low(k):
        return g % (2 << k) == 0

    def is_high(k):
        return g % (2 << k) == (1 << k)

    loads = {}
    for name, source, target in (
        ("tv", tv_hbm, tv_ref),
        ("tt", tt_hbm, tt_ref),
        ("lv", lv_hbm, lv_ref),
        ("c0", c_hbm.at[:, pl.ds(0, b)], c_ref.at[:, pl.ds(0, b)]),
        ("lt", lt_hbm, lt_ref),
        ("c1", c_hbm.at[:, pl.ds(b, nc - b)], c_ref.at[:, pl.ds(b, nc - b)]),
        ("inv", inv_hbm, inv_ref),
    ):
        loads[name] = pltpu.make_async_copy(source, target, local_sems.at[len(loads)])
        loads[name].start()

    barrier = pltpu.get_barrier_semaphore()

    def greet(other):
        pl.semaphore_signal(barrier, inc=1, device_id=(other,), device_id_type=MESH)

    met = []

    def meet(condition, other):
        @pl.when(condition)
        def _():
            greet(other)

        met.append(condition)

    for j in range(1, ROW):
        greet(base + (r + j) % ROW)
    for k in range(row_levels):
        meet(is_low(k), me + (ROW << k))
        meet(is_high(k), me - (ROW << k))
    for z in range(1, zdim):
        if z & (z - 1):
            meet(g == 0, me + z * YDIM * ROW)
            meet(g == z * YDIM, me - z * YDIM * ROW)
    meet(y == 0, me + 3 * ROW)
    meet(y == 3, me - 3 * ROW)

    def entered():
        peers = ROW - 1
        for condition in met:
            peers = peers + condition.astype(jnp.int32)
        pl.semaphore_wait(barrier, peers)

    numbers = {}
    pending = []

    def number(*name):
        return numbers.setdefault(name, len(numbers))

    def remote(source, target, receive, other):
        return pltpu.make_async_remote_copy(
            src_ref=source,
            dst_ref=target,
            send_sem=send_sem,
            recv_sem=recv_sems.at[receive],
            device_id=(other,),
            device_id_type=MESH,
        )

    def copy(source, target, name, other, condition=None):
        remote(source, target, number(*name), other).start()
        pending.append((condition, source))

    def arrived(target, name):
        remote(target, target, number(*name), neighbour).wait_recv()

    row_id = lax.broadcasted_iota(jnp.int32, (b, b), 0)
    col_id = lax.broadcasted_iota(jnp.int32, (b, b), 1)
    row_half = lax.broadcasted_iota(jnp.int32, (hb, hb), 0)
    col_half = lax.broadcasted_iota(jnp.int32, (hb, hb), 1)

    def t_of(ref):
        return jnp.where(row_id <= col_id, ref[:b, :], 0.0)

    def vt_of(ref):
        diagonal = jnp.where(row_id == col_id, ref[b : b + 1, :], 0.0)
        return jnp.where(row_id > col_id, ref[:b, :], diagonal)

    def make_fold(target, t):
        last = t[hb:, hb:]
        target[:hb, :hb] = jnp.where(row_half <= col_half, t[:hb, :hb], last.T)
        target[:hb, hb:] = t[:hb, hb:]
        diagonal = jnp.sum(
            jnp.where(row_half == col_half, last, 0.0), axis=0, keepdims=True
        )
        target[hb:, :hb] = jnp.broadcast_to(diagonal, (8, hb))
        target[hb:, hb:] = jnp.zeros((8, hb), F32)

    def store_t(index, value, rows, columns):
        high, low = halves(value)
        t_high[index, rows, columns] = high
        t_low[index, rows, columns] = low

    FIRST, LAST = pl.ds(0, hb), pl.ds(hb, hb)

    def t_from_fold(index):
        first = fold[index, :hb, :hb]
        store_t(index, jnp.where(row_half <= col_half, first, 0.0), FIRST, FIRST)
        store_t(index, fold[index, :hb, hb:], FIRST, LAST)
        store_t(index, jnp.zeros((hb, hb), F32), LAST, FIRST)
        diagonal = jnp.where(row_half == col_half, fold[index, hb : hb + 1, :hb], 0.0)
        last = jnp.where(row_half < col_half, first.T, diagonal)
        store_t(index, last, LAST, LAST)

    def t_from_slot(index):
        store_t(index, t_of(slot[index]), pl.ds(0, b), pl.ds(0, b))

    def make_bt(index):
        high, low = halves(dot3(vt_of(slot[index]).T, t_of(slot[index])))
        bt_high[index] = high
        bt_low[index] = low

    def times_bt(value, index):
        return dot_pairs(halves(value), (bt_high[index], bt_low[index]))

    def times_t(value, index):
        return dot_pairs(halves(value), (t_high[index], t_low[index]))

    loads["tv"].wait()
    loads["tt"].wait()
    tv = tv_ref[...]
    tt = tt_ref[...]
    pack[:b, :] = jnp.where(row_id <= col_id, tt, tv.T)
    diagonal = jnp.sum(jnp.where(row_id == col_id, tv, 0.0), axis=0, keepdims=True)
    pack[b:, :] = jnp.broadcast_to(diagonal, (8, b))
    make_fold(folded, tt)

    for condition, index in (
        (core == 1, 0), ((r == 2) | (r == 6), 1), (r == 4, 2), ((r == 0) & (g > 0), 3),
    ):
        @pl.when(condition)
        def _():
            slot[index][...] = pack[...]
            make_bt(index)
            if index < 3:
                t_from_slot(index)

    loads["lv"].wait()
    high, low = halves(lv_ref[...].T)
    lvt_high[...] = high
    lvt_low[...] = low

    def leaf_tile(tile):
        columns = pl.ds(tile * b, b)
        inner = dot_pairs((lvt_high[...], lvt_low[...]), halves(c_ref[:, columns]))
        coeffs = dot3(lt_ref[...].T, inner)
        coef[:, columns] = coeffs
        result = c_ref[:b, columns] - dot3(lv_ref[:b, :], coeffs)
        head[columns, :] = result.T

    loads["c0"].wait()
    loads["lt"].wait()
    leaf_tile(0)
    entered()

    @pl.when(core == 1)
    def _():
        copy(folded, folds[0], ("fold", 0), me - 1, lambda: core == 1)

    @pl.when((r == 2) | (r == 6))
    def _():
        c = lambda: (r == 2) | (r == 6)
        copy(pack, slot1, ("slot", 1), me + 1, c)
        copy(folded, folds[1], ("fold", 1), me - 2, c)

    @pl.when(r == 4)
    def _():
        copy(pack, slot2, ("slot", 2), base + 5, lambda: r == 4)
        copy(folded, folds[2], ("fold", 2), base + 2, lambda: r == 4)
        copy(pack, slot2, ("slot", 2), base + 6, lambda: r == 4)

    @pl.when((r == 0) & (g > 0))
    def _():
        for other in (1, 2, 6):
            copy(pack, slot3, ("slot", 3), base + other, lambda: (r == 0) & (g > 0))

    def send(level, chunk):
        bit, far = bits[level], 1 << level
        rows, name = own(level, chunk), ("x", level, chunk)
        target = ins[level].at[rows, :]
        low_rows, high_rows = part(level, chunk, False), part(level, chunk, True)

        @pl.when(bit == 0)
        def _():
            copy(
                parent(level).at[high_rows, :], target, name, me + far,
                lambda: bits[level] == 0,
            )

        source = zs[level].at[rows, :]

        @pl.when(bit == 1)
        def _():
            zs[level][rows, :] = times_bt(parent(level)[low_rows, :], level)
            copy(source, target, name, me - far, lambda: bits[level] == 1)

    def finish(level, chunk):
        bit = bits[level]
        rows, name = own(level, chunk), ("x", level, chunk)
        low_rows, high_rows = part(level, chunk, False), part(level, chunk, True)

        @pl.when(bit == 0)
        def _():
            value = parent(level)[low_rows, :]
            update = times_t(value, level)
            arrived(ins[level].at[rows, :], name)
            update = update + ins[level][rows, :]
            cur[level][rows, :] = value - update
            ws[level][rows, :] = update

        @pl.when(bit == 1)
        def _():
            update = times_bt(parent(level)[high_rows, :], level)
            arrived(ins[level].at[rows, :], name)
            value = ins[level][rows, :]
            update = update + times_t(value, level)
            cur[level][rows, :] = value - update
            ws[level][rows, :] = update

    def give_back(level, chunk):
        rows = own(level, chunk)

        @pl.when(bits[level] == 0)
        def _():
            copy(
                ws[level].at[rows, :], wbs[level].at[rows, :], ("w", level, chunk),
                me + (1 << level), lambda: bits[level] == 0,
            )

    def residual(level, result):
        @pl.when(bits[level] == 1)
        def _():
            vt = halves(vt_of(slot[level]))
            for chunk in CHUNKS:
                rows = own(level, chunk)
                low_rows, high_rows = part(level, chunk, False), part(level, chunk, True)
                result[high_rows, :] = parent(level)[high_rows, :] - dot_pairs(
                    halves(ws[level][rows, :]), vt
                )
                arrived(wbs[level].at[rows, :], ("w", level, chunk))
                result[low_rows, :] = parent(level)[low_rows, :] - dot_pairs(
                    halves(wbs[level][rows, :]), vt
                )

    def place(level, rank, chunk):
        start = b if chunk else 0
        for bit in range(level):
            start += (rank >> bit & 1) * size(bit, chunk)
        return pl.ds(start, size(level - 1, chunk))

    def buffer_rows(level, chunk):
        return pl.ds((b >> level) if chunk else 0, size(level - 1, chunk))

    def gather(level, result, rank, into, chunks, condition):
        for chunk in chunks:
            if rank == into:
                gathered[place(level, rank, chunk), :] = result[buffer_rows(level, chunk), :]
            else:
                copy(
                    result.at[buffer_rows(level, chunk), :],
                    gathered.at[place(level, rank, chunk), :],
                    ("gather",), base + into, condition,
                )

    send(0, 0)
    loads["c1"].wait()
    for tile in range(1, nc // b):
        leaf_tile(tile)
    send(0, 1)

    @pl.when(core == 0)
    def _():
        arrived(folds[0], ("fold", 0))
        t_from_fold(0)

    finish(0, 0)

    @pl.when((r == 3) | (r == 7))
    def _():
        arrived(slot1, ("slot", 1))
        make_bt(1)
        t_from_slot(1)

    send(1, 0)

    @pl.when(r == 4)
    def _():
        copy(folded, folds[2], ("fold", 2), base, lambda: r == 4)

    finish(0, 1)
    send(1, 1)

    @pl.when((r == 0) & (g > 0))
    def _():
        copy(pack, slot3, ("slot", 3), base + 4, lambda: (r == 0) & (g > 0))

    @pl.when((r == 0) | (r == 4))
    def _():
        arrived(folds[1], ("fold", 1))
        copy(folds[1], folds[1], ("fold", 1), me + 1, lambda: (r == 0) | (r == 4))
        t_from_fold(1)

    give_back(0, 0)
    give_back(0, 1)

    @pl.when(r == 6)
    def _():
        arrived(slot2, ("slot", 2))
        copy(slot2, slot2, ("slot", 2), me + 1, lambda: r == 6)
        make_bt(2)
        t_from_slot(2)

    @pl.when((r == 5) | (r == 7))
    def _():
        arrived(slot2, ("slot", 2))
        make_bt(2)
        t_from_slot(2)

    @pl.when((r == 1) | (r == 5))
    def _():
        arrived(folds[1], ("fold", 1))
        t_from_fold(1)

    finish(1, 0)
    send(2, 0)

    @pl.when((r == 0) | (r == 2))
    def _():
        arrived(folds[2], ("fold", 2))
        copy(folds[2], folds[2], ("fold", 2), me + 1, lambda: (r == 0) | (r == 2))
        t_from_fold(2)

    finish(1, 1)
    send(2, 1)

    @pl.when((g > 0) & (core == 0))
    def _():
        @pl.when(r > 0)
        def _():
            arrived(slot3, ("slot", 3))
            copy(
                slot3, slot3, ("slot", 3), me + 1,
                lambda: (g > 0) & (core == 0) & (r > 0),
            )

        make_fold(row_fold, t_of(slot3))
        for k in range(row_levels):
            @pl.when(is_high(k))
            def _():
                copy(
                    row_fold, folds[3 + k], ("fold", 3 + k), me - (ROW << k),
                    functools.partial(lambda k: is_high(k) & (core == 0), k),
                )

    give_back(1, 0)
    give_back(1, 1)

    @pl.when((r == 1) | (r == 3))
    def _():
        arrived(folds[2], ("fold", 2))
        t_from_fold(2)

    def rest_tile(tile):
        columns = pl.ds(tile * b, b)
        rest[:, columns] = c_ref[b:, columns] - dot3(lv_ref[b:, :], coef[:, columns])

    rest_tile(0)
    loads["inv"].wait()
    rest_basis[...] = dot3(rest[:, :b], inv_ref[...])
    for tile in range(1, nc // b):
        rest_tile(tile)
    local = [
        pltpu.make_async_copy(rest, upd_out.at[pl.ds(b, b), :], local_sems.at[7]),
        pltpu.make_async_copy(rest_basis, basis_out.at[pl.ds(b, b), :], local_sems.at[8]),
    ]
    for made in local:
        made.start()

    @pl.when((g > 0) & (core == 1))
    def _():
        arrived(slot3, ("slot", 3))

    @pl.when((g > 0) & (r > 0))
    def _():
        make_bt(3)

    def send_row(k, chunk):
        rows = ROW_CHUNKS[chunk]
        source = zr.at[rows, :]

        @pl.when(is_high(k))
        def _():
            zr[rows, :] = times_bt(cur2[rows, :], 3)
            copy(
                source, inr.at[k, rows, :], ("z", k, chunk), me - (ROW << k),
                functools.partial(is_high, k),
            )

    def finish_row(k, chunk):
        rows = ROW_CHUNKS[chunk]
        source = wr.at[k, rows, :]

        @pl.when(is_low(k))
        def _():
            value = cur2[rows, :]
            update = times_t(value, 3 + k)
            arrived(inr.at[k, rows, :], ("z", k, chunk))
            update = update + inr[k, rows, :]
            cur2[rows, :] = value - update
            wr[k, rows, :] = update
            copy(
                source, wbr.at[rows, :], ("wr", chunk), me + (ROW << k),
                functools.partial(is_low, k),
            )

    def row_operators(k):
        @pl.when(is_low(k))
        def _():
            arrived(folds[3 + k], ("fold", 3 + k))

            @pl.when(core == 0)
            def _():
                copy(
                    folds[3 + k], folds[3 + k], ("fold", 3 + k), me + 1,
                    functools.partial(lambda k: is_low(k) & (core == 0), k),
                )

            t_from_fold(3 + k)

    finish(2, 0)
    send_row(0, 0)
    finish(2, 1)
    send_row(0, 1)
    send_row(0, 2)
    give_back(2, 0)
    give_back(2, 1)

    columns = c_ref[:, :b]
    gram_own[...] = dot3(columns.T, columns)
    for j in range(1, ROW):
        other = (r + j) % ROW
        copy(
            gram_own.at[piece_of(other), :], gram_in.at[ROW - j - 1],
            ("gram",), base + other,
        )

    def chain(k):
        @pl.when(is_high(k))
        def _():
            copy(
                gram_piece, gram_level.at[k], ("level", k), me - (ROW << k),
                functools.partial(is_high, k),
            )

        @pl.when(is_low(k))
        def _():
            arrived(gram_level.at[k], ("level", k))
            gram_piece[...] = gram_piece[...] + gram_level[k]

    def gram_sum():
        arrived(gram_in, ("gram",))
        total = gram_own[mine, :]
        for j in range(ROW - 1):
            total = total + gram_in[j]
        gram_piece[...] = total

    def panel_out():
        @pl.when(g == 0)
        def _():
            panel[mine, :] = cur2[ROW_CHUNKS[0], :]
            for j in range(1, ROW):
                copy(
                    cur2.at[ROW_CHUNKS[0], :], panel.at[mine, :],
                    ("panel",), base + (r + j) % ROW, lambda: g == 0,
                )

    def gram_out_z():
        @pl.when(g == 0)
        def _():
            arrived(panel.at[pl.ds(0, b - piece), :], ("panel",))
            square = dot3(panel[mine, :], panel[...], True)
            gram_all[mine, :] = (gram_piece[...] - square) / float(total_rows)
            for z in range(1, zdim):
                copy(
                    gram_all.at[mine, :], gram_all.at[mine, :], ("gz",),
                    me + z * YDIM * ROW, lambda: g == 0,
                )

    events = []
    for k in range(row_levels):
        events += [(2.9 * k, k, 0), (2.0 + 4.2 * k, k, 1), (2.9 + 4.2 * k, k, 2)]
    done = set()
    last = row_levels - 1
    for _, k, chunk in sorted(events):
        if chunk == 0:
            row_operators(k)
        finish_row(k, chunk)
        if k < last:
            send_row(k + 1, chunk)
        done.add((k, chunk))
        if (k, chunk) == (last, 0):
            panel_out()
        if (k, chunk) == (0, 2):
            residual(0, gathered)
            residual(1, res1)
            for rank, into in ((2, 2), (3, 2), (6, 6), (7, 6)):
                @pl.when(r == rank)
                def _():
                    gather(1, res1, rank, into, CHUNKS, functools.partial(lambda o: r == o, rank))
        if (k, chunk) == (1, 2):
            residual(2, res2)
            for rank in range(4, ROW):
                @pl.when(r == rank)
                def _():
                    gather(2, res2, rank, 4, CHUNKS, functools.partial(lambda o: r == o, rank))
            gram_sum()
            chain(0)
            chain(1)
        if (k, chunk) == (2, 2):
            chain(2)
            if last > 2:
                chain(3)
        if last > 3 and (k, chunk) == (4, 0):
            chain(4)
        if last > 3 and (k, chunk) == (last - 1, 2):
            gram_out_z()
    if last <= 3:
        gram_out_z()

    def row_result(condition):
        @pl.when(condition())
        def _():
            vt = halves(vt_of(slot3))
            for chunk, rows in enumerate(ROW_CHUNKS):
                arrived(wbr.at[rows, :], ("wr", chunk))
                res3[rows, :] = cur2[rows, :] - dot_pairs(halves(wbr[rows, :]), vt)
                if chunk == 1:
                    continue
                for rank in range(ROW):
                    @pl.when(r == rank)
                    def _():
                        gather(
                            3, res3, rank, 0, (min(chunk, 1),),
                            functools.partial(lambda o: condition() & (r == o), rank),
                        )

    half_way = row_count // 2
    row_result(lambda: (g > 0) & (g != half_way))

    @pl.when(g == 0)
    def _():
        for rank in range(ROW):
            @pl.when(r == rank)
            def _():
                gather(
                    3, cur2, rank, 0, CHUNKS,
                    functools.partial(lambda o: (g == 0) & (r == o), rank),
                )

    @pl.when(y == 0)
    def _():
        @pl.when(g > 0)
        def _():
            arrived(gram_all.at[mine, :], ("gz",))

        for step in range(1, YDIM):
            copy(
                gram_all.at[mine, :], gram_all.at[mine, :], ("gy",),
                me + step * ROW, lambda: y == 0,
            )

    row_result(lambda: g == half_way)

    @pl.when(y != 0)
    def _():
        arrived(gram_all.at[mine, :], ("gy",))

    for j in range(1, ROW):
        copy(
            gram_all.at[mine, :], gram_all.at[mine, :], ("gx",),
            base + (r + j) % ROW,
        )

    @pl.when((r == 2) | (r == 6))
    def _():
        arrived(gathered.at[pl.ds(0, nc // 2), :], ("gather",))

    @pl.when(r == 4)
    def _():
        arrived(gathered.at[pl.ds(0, 3 * nc // 4), :], ("gather",))

    @pl.when(r == 0)
    def _():
        arrived(gathered.at[pl.ds(0, 7 * nc // 8), :], ("gather",))

    head_rows[...] = gathered[...].T
    head_basis[...] = jnp.where(me == 0, 0.0, dot3(head_rows[:, :b], inv_ref[...]))
    local += [
        pltpu.make_async_copy(head_rows, upd_out.at[pl.ds(0, b), :], local_sems.at[9]),
        pltpu.make_async_copy(head_basis, basis_out.at[pl.ds(0, b), :], local_sems.at[10]),
    ]
    for made in local[2:]:
        made.start()
    arrived(gram_all.at[pl.ds(0, b - piece), :], ("gx",))
    local.append(pltpu.make_async_copy(gram_all, gram_out, local_sems.at[11]))
    local[-1].start()

    for condition, source in pending:
        made = functools.partial(
            lambda source: remote(source, source, 0, neighbour).wait_send(), source
        )
        if condition is None:
            made()
        else:
            @pl.when(condition())
            def _():
                made()
    for made in local:
        made.wait()
    assert len(numbers) <= recv_sems.shape[0]


def body(trailing, leaf_vectors, leaf_factors, tree_vectors, tree_factors, inverse_factor):
    b, nc = leaf_vectors.shape[1], trailing.shape[1]
    devices = lax.axis_size("rows")
    total_rows = trailing.shape[0] * devices
    levels = (devices // ROW).bit_length() - 1
    piece = b // ROW

    def vmem(*shape, dtype=F32):
        return pltpu.VMEM(shape, dtype)

    arguments = (
        trailing, leaf_vectors, leaf_factors, tree_vectors, tree_factors, inverse_factor
    )
    per_level = [vmem(nc >> level, b) for level in (1, 2, 3)]
    scratch = [
        *[vmem(*argument.shape) for argument in arguments],
        vmem(b + 8, b),
        vmem(b // 2 + 8, b),
        *[vmem(b + 8, b)] * 4,
        vmem(3 + levels, b // 2 + 8, b),
        vmem(b // 2 + 8, b),
        vmem(3 + levels, b, b, dtype=BF16),
        vmem(3 + levels, b, b, dtype=BF16),
        vmem(4, b, b, dtype=BF16),
        vmem(4, b, b, dtype=BF16),
        vmem(nc, b),
        *per_level,
        *per_level, *per_level, *per_level, *per_level,
        vmem(nc // 8, b), vmem(levels, nc // 8, b), vmem(levels, nc // 8, b),
        vmem(nc // 8, b),
        *per_level,
        vmem(nc, b),
        vmem(b, nc), vmem(b, nc), vmem(b, b), vmem(b, nc), vmem(b, b),
        vmem(b, 2 * b, dtype=BF16), vmem(b, 2 * b, dtype=BF16),
        vmem(b, b), vmem(ROW - 1, piece, b), vmem(piece, b), vmem(levels, piece, b),
        vmem(b, b), vmem(b, b),
        pltpu.SemaphoreType.DMA,
        pltpu.SemaphoreType.DMA((RECEIVES,)),
        pltpu.SemaphoreType.DMA((12,)),
    ]
    return pl.pallas_call(
        functools.partial(tree_kernel, devices, total_rows),
        out_shape=(
            jax.ShapeDtypeStruct(trailing.shape, F32),
            jax.ShapeDtypeStruct(leaf_vectors.shape, F32),
            jax.ShapeDtypeStruct((b, b), F32),
        ),
        in_specs=[pl.BlockSpec(memory_space=pl.ANY)] * 6,
        out_specs=[pl.BlockSpec(memory_space=pl.ANY)] * 3,
        scratch_shapes=scratch,
        compiler_params=pltpu.CompilerParams(
            collective_id=0,
            has_side_effects=True,
            vmem_limit_bytes=56 * 1024 * 1024,
        ),
        name="tree",
    )(*arguments)


def solution(mesh):
    rows = P("rows", None)
    return jax.shard_map(
        body,
        mesh=mesh,
        in_specs=(rows, rows, rows, rows, rows, P()),
        out_specs=(rows, rows, P()),
        check_vma=False,
    )
```

time: 87.6 us -> 74 us (0.84)
  the two profiles are of different devices: /device:TPU:49 before, /device:TPU:129 now
where the time goes in v3:
time: 74 us; the launch traced here: 73.9 us
  Pallas kernels  68.5 us (93%)
  local copies, waits for them, and re-layouts  4.73 us (6%)
    pallas_call x1, Pallas kernels, body(): pl.pallas_call(functools.partial(tree_kernel, devices, total_rows), out_s...  68.5 us
    unnamed x7, local copies, waits for them, and re-layouts  4.73 us

profile of v3, /device:TPU:129, one launch (start us, length us, event | category | flops | bytes accessed | tf_op | source)
XLA Modules:
  0.0 73.9 jit_solution(4048673115053643548)
XLA Ops:
  0.6 68.5 %tree.1 = (f32[512,1024]{1,0:T(8,128)}, f32[512,256]{1,0:T(8,128)}, f32[256,256]{1,0:T(8,128)}) custom-call(f32[512,1024]{1,0:T(8,128)} %c_hbm.1, f32[512,256]{1,0:T(8,128)} %lv_hbm.1, f32[256,256]{1,0:T(8,128)} %lt_hbm.1, f32[256,256]{1,0:T(8,128)} %tv_hbm.1, f32[256,256]{1,0:T(8,128)} %tt_hbm.1, f32[256,256]{1,0:T(8,128)} %inv_hbm.1), custom_call_target="tpu_custom_call" | custom-call | tf_op jit(solution)/shard_map/tree/pallas_call | solution.py:781
  69.2 0.0 copy-start
  69.2 0.0 copy-start.1
  69.2 3.2 %copy.12 = f32[512,1024]{1,0:T(8,128)} copy(f32[512,1024]{1,0:T(8,128)} %get-tuple-element.6) | data formatting | bytes 4194304
  72.4 0.0 copy-done
  72.4 0.8 %copy.13 = f32[512,256]{1,0:T(8,128)} copy(f32[512,256]{1,0:T(8,128)S(1)} %copy-done) | data formatting | bytes 1048576
  73.2 0.0 copy-done.1
  73.2 0.7 copy.14
Async XLA Ops:
  69.2 3.3 %copy-start = (f32[512,256]{1,0:T(8,128)S(1)}, f32[512,256]{1,0:T(8,128)}, u32[]{:S(2)}) copy-start(f32[512,256]{1,0:T(8,128)} %get-tuple-element.7) | copy-start | bytes 1572868
  69.2 4.0 %copy-start.1 = (f32[256,256]{1,0:T(8,128)S(1)}, f32[256,256]{1,0:T(8,128)}, u32[]{:S(2)}) copy-start(f32[256,256]{1,0:T(8,128)} %get-tuple-element.8) | copy-start | bytes 786436

commit v4 on v3

--- a/solution.py
+++ b/solution.py
@@ -44,7 +44,7 @@
     folded,
     slot0, slot1, slot2, slot3,
     fold,
-    row_fold,
+    row_fold, row_fold_bt,
     t_high, t_low,
     bt_high, bt_low,
     head,
@@ -55,7 +55,7 @@
     gathered,
     coef, rest, rest_basis, head_rows, head_basis,
     lvt_high, lvt_low,
-    gram_own, gram_in, gram_piece, gram_level, panel, gram_all,
+    gram_own, gram_piece, gram_y, gram_z, gram_x, panel, gram_all, gram_total, wback,
     send_sem, recv_sems, local_sems,
 ):
     b = pack.shape[1]
@@ -74,7 +74,15 @@
     bits = (core, x0, x1)
     base = g * ROW
     y = g % YDIM
+    z = g // YDIM
     neighbour = base + (r + 1) % ROW
+
+    def y_mate(j):
+        return (z * YDIM + (y + j) % YDIM) * ROW + r
+
+    def z_mate(j):
+        return ((z + j) % zdim * YDIM + y) * ROW + r
+
     cur = (cur0, cur1, cur2)
     zs, ins, ws, wbs = (z0, z1, z2), (in0, in1, in2), (w0, w1, w2), (wb0, wb1, wb2)
     slot = (slot0, slot1, slot2, slot3)
@@ -113,6 +121,17 @@
 
     def is_high(k):
         return g % (2 << k) == (1 << k)
+
+    def low_half(k):
+        return is_low(k) if k < 2 else (y == 0) & (g // (1 << k) % 2 == 0)
+
+    def high_half(k):
+        return is_high(k) if k < 2 else (y == 0) & (g // (1 << k) % 2 == 1)
+
+    def takes_fold(k):
+        return is_low(k) if k < 2 else (y == 0) & jnp.logical_not(is_high(k))
+
+    backs = [wback.at[k] for k in range(row_levels)]
 
     loads = {}
     for name, source, target in (
@@ -132,32 +151,15 @@
     def greet(other):
         pl.semaphore_signal(barrier, inc=1, device_id=(other,), device_id_type=MESH)
 
-    met = []
-
-    def meet(condition, other):
-        @pl.when(condition)
-        def _():
-            greet(other)
-
-        met.append(condition)
-
     for j in range(1, ROW):
         greet(base + (r + j) % ROW)
-    for k in range(row_levels):
-        meet(is_low(k), me + (ROW << k))
-        meet(is_high(k), me - (ROW << k))
-    for z in range(1, zdim):
-        if z & (z - 1):
-            meet(g == 0, me + z * YDIM * ROW)
-            meet(g == z * YDIM, me - z * YDIM * ROW)
-    meet(y == 0, me + 3 * ROW)
-    meet(y == 3, me - 3 * ROW)
+    for j in range(1, YDIM):
+        greet(y_mate(j))
+    for j in range(1, zdim):
+        greet(z_mate(j))
 
     def entered():
-        peers = ROW - 1
-        for condition in met:
-            peers = peers + condition.astype(jnp.int32)
-        pl.semaphore_wait(barrier, peers)
+        pl.semaphore_wait(barrier, ROW - 1 + YDIM - 1 + zdim - 1)
 
     numbers = {}
     pending = []
@@ -283,6 +285,7 @@
 
     @pl.when(r == 4)
     def _():
+        copy(folded, folds[2], ("fold", 2), base, lambda: r == 4)
         copy(pack, slot2, ("slot", 2), base + 5, lambda: r == 4)
         copy(folded, folds[2], ("fold", 2), base + 2, lambda: r == 4)
         copy(pack, slot2, ("slot", 2), base + 6, lambda: r == 4)
@@ -380,6 +383,71 @@
                     ("gather",), base + into, condition,
                 )
 
+    yrows, zrows = b // YDIM, b // YDIM // zdim
+
+    def block_y(other):
+        return pl.ds(pl.multiple_of(other * yrows, yrows), yrows)
+
+    def block_z(other):
+        return pl.ds(pl.multiple_of(other * zrows, zrows), zrows)
+
+    my_rows = pl.ds(pl.multiple_of(y * yrows + z * zrows, zrows), zrows)
+
+    def gram_start():
+        columns = c_ref[:, :b]
+        gram_own[...] = dot3(columns.T, columns)
+        for j in range(1, YDIM):
+            copy(
+                gram_own.at[block_y((y + j) % YDIM), :], gram_y.at[YDIM - j - 1],
+                ("gram y",), y_mate(j),
+            )
+
+    def gram_sum_y():
+        arrived(gram_y, ("gram y",))
+        total = gram_own[block_y(y), :]
+        for j in range(YDIM - 1):
+            total = total + gram_y[j]
+        gram_piece[...] = total
+        for j in range(1, zdim):
+            copy(
+                gram_piece.at[block_z((z + j) % zdim), :], gram_z.at[zdim - j - 1],
+                ("gram z",), z_mate(j),
+            )
+
+    mine_x = gram_x.at[r]
+
+    def gram_sum_z():
+        total = gram_piece[block_z(z), :]
+        if zdim > 1:
+            arrived(gram_z, ("gram z",))
+        for j in range(zdim - 1):
+            total = total + gram_z[j]
+        gram_x[r] = total
+        for j in range(1, ROW):
+            copy(
+                mine_x, mine_x, ("gram x",), base + (r + j) % ROW,
+            )
+
+    def gram_sum_x():
+        arrived(gram_x.at[pl.ds(0, ROW - 1)], ("gram x",))
+        total = gram_x[0]
+        for j in range(1, ROW):
+            total = total + gram_x[j]
+        gram_all[my_rows, :] = total
+        for j in range(1, zdim):
+            copy(
+                gram_all.at[my_rows, :], gram_all.at[my_rows, :], ("all z",), z_mate(j),
+            )
+
+    def gram_all_y():
+        if zdim > 1:
+            arrived(gram_all.at[pl.ds(0, yrows - zrows), :], ("all z",))
+        for j in range(1, YDIM):
+            copy(
+                gram_all.at[block_y(y), :], gram_all.at[block_y(y), :], ("all y",),
+                y_mate(j),
+            )
+
     send(0, 0)
     loads["c1"].wait()
     for tile in range(1, nc // b):
@@ -401,10 +469,6 @@
 
     send(1, 0)
 
-    @pl.when(r == 4)
-    def _():
-        copy(folded, folds[2], ("fold", 2), base, lambda: r == 4)
-
     finish(0, 1)
     send(1, 1)
 
@@ -420,6 +484,7 @@
 
     give_back(0, 0)
     give_back(0, 1)
+    gram_start()
 
     @pl.when(r == 6)
     def _():
@@ -462,13 +527,25 @@
             )
 
         make_fold(row_fold, t_of(slot3))
+
+        @pl.when(r > 0)
+        def _():
+            make_bt(3)
+
+        if row_levels > 2:
+            make_fold(row_fold_bt, bt_high[3].astype(F32) + bt_low[3].astype(F32))
         for k in range(row_levels):
             @pl.when(is_high(k))
             def _():
-                copy(
-                    row_fold, folds[3 + k], ("fold", 3 + k), me - (ROW << k),
-                    functools.partial(lambda k: is_high(k) & (core == 0), k),
-                )
+                c = functools.partial(lambda k: is_high(k) & (core == 0), k)
+                name = ("fold", 3 + k)
+                for j in range(max(1, (1 << k) // YDIM)):
+                    copy(
+                        row_fold, folds[3 + k], name,
+                        me - (ROW << k) + j * YDIM * ROW, c,
+                    )
+                    if j:
+                        copy(row_fold_bt, folds[3 + k], name, me + j * YDIM * ROW, c)
 
     give_back(1, 0)
     give_back(1, 1)
@@ -482,6 +559,7 @@
         columns = pl.ds(tile * b, b)
         rest[:, columns] = c_ref[b:, columns] - dot3(lv_ref[b:, :], coef[:, columns])
 
+    gram_sum_y()
     rest_tile(0)
     loads["inv"].wait()
     rest_basis[...] = dot3(rest[:, :b], inv_ref[...])
@@ -498,11 +576,11 @@
     def _():
         arrived(slot3, ("slot", 3))
 
-    @pl.when((g > 0) & (r > 0))
+    @pl.when((g > 0) & (core == 1))
     def _():
         make_bt(3)
 
-    def send_row(k, chunk):
+    def send_z(k, chunk):
         rows = ROW_CHUNKS[chunk]
         source = zr.at[rows, :]
 
@@ -514,95 +592,156 @@
                 functools.partial(is_high, k),
             )
 
+    def send_u(k, chunk):
+        rows = ROW_CHUNKS[chunk]
+        ahead = wr.at[k, rows, :]
+
+        @pl.when(is_low(k))
+        def _():
+            wr[k, rows, :] = times_t(cur2[rows, :], 3 + k)
+            copy(
+                ahead, wbr.at[rows, :], ("wr", chunk), me + (ROW << k),
+                functools.partial(is_low, k),
+            )
+
     def finish_row(k, chunk):
         rows = ROW_CHUNKS[chunk]
-        source = wr.at[k, rows, :]
 
         @pl.when(is_low(k))
         def _():
-            value = cur2[rows, :]
-            update = times_t(value, 3 + k)
             arrived(inr.at[k, rows, :], ("z", k, chunk))
-            update = update + inr[k, rows, :]
-            cur2[rows, :] = value - update
-            wr[k, rows, :] = update
-            copy(
-                source, wbr.at[rows, :], ("wr", chunk), me + (ROW << k),
+            cur2[rows, :] = cur2[rows, :] - (wr[k, rows, :] + inr[k, rows, :])
+
+    PANEL = ROW_CHUNKS[0]
+
+    def send_shared(k):
+        ours = wr.at[k, PANEL, :]
+
+        @pl.when(low_half(k))
+        def _():
+            value = cur2[PANEL, :]
+            wr[k, PANEL, :] = value - times_t(value, 3 + k)
+            copy(
+                ours, inr.at[k, PANEL, :], ("z", k, 0), me + (ROW << k),
+                functools.partial(low_half, k),
+            )
+
+        @pl.when(high_half(k))
+        def _():
+            wr[k, PANEL, :] = -times_t(cur2[PANEL, :], 3 + k)
+            copy(
+                ours, inr.at[k, PANEL, :], ("z", k, 0), me - (ROW << k),
+                functools.partial(high_half, k),
+            )
+
+    def finish_shared(k):
+        back = backs[k]
+
+        @pl.when(y == 0)
+        def _():
+            arrived(inr.at[k, PANEL, :], ("z", k, 0))
+
+        @pl.when(is_high(k))
+        def _():
+            res3[PANEL, :] = cur2[PANEL, :]
+
+        @pl.when(is_low(k))
+        def _():
+            value = cur2[PANEL, :] - (wr[k, PANEL, :] + inr[k, PANEL, :])
+            wback[k, :, :] = value
+            copy(
+                back, wbr.at[PANEL, :], ("wr", 0), me + (ROW << k),
                 functools.partial(is_low, k),
             )
 
+        @pl.when(y == 0)
+        def _():
+            cur2[PANEL, :] = wr[k, PANEL, :] + inr[k, PANEL, :]
+
+    def send_level(k, chunk):
+        if k > 1 and chunk == 0:
+            send_shared(k)
+        else:
+            send_z(k, chunk)
+            send_u(k, chunk)
+
+    def finish_level(k, chunk):
+        if k > 1 and chunk == 0:
+            finish_shared(k)
+        else:
+            finish_row(k, chunk)
+
+    def forward_operators(k):
+        @pl.when(takes_fold(k) & (core == 0))
+        def _():
+            arrived(folds[3 + k], ("fold", 3 + k))
+            copy(
+                folds[3 + k], folds[3 + k], ("fold", 3 + k), me + 1,
+                functools.partial(lambda k: takes_fold(k) & (core == 0), k),
+            )
+
     def row_operators(k):
-        @pl.when(is_low(k))
+        @pl.when(takes_fold(k) & (core == 1))
         def _():
             arrived(folds[3 + k], ("fold", 3 + k))
 
-            @pl.when(core == 0)
+        if k > 1:
+            @pl.when(is_high(k))
             def _():
-                copy(
-                    folds[3 + k], folds[3 + k], ("fold", 3 + k), me + 1,
-                    functools.partial(lambda k: is_low(k) & (core == 0), k),
-                )
-
+                make_fold(fold.at[3 + k], bt_high[3].astype(F32) + bt_low[3].astype(F32))
+
+        @pl.when(takes_fold(k) if k < 2 else y == 0)
+        def _():
             t_from_fold(3 + k)
 
     finish(2, 0)
-    send_row(0, 0)
+    send_z(0, 0)
     finish(2, 1)
-    send_row(0, 1)
-    send_row(0, 2)
+    send_z(0, 1)
+    send_z(0, 2)
+    forward_operators(0)
     give_back(2, 0)
     give_back(2, 1)
 
-    columns = c_ref[:, :b]
-    gram_own[...] = dot3(columns.T, columns)
-    for j in range(1, ROW):
-        other = (r + j) % ROW
-        copy(
-            gram_own.at[piece_of(other), :], gram_in.at[ROW - j - 1],
-            ("gram",), base + other,
-        )
-
-    def chain(k):
-        @pl.when(is_high(k))
-        def _():
-            copy(
-                gram_piece, gram_level.at[k], ("level", k), me - (ROW << k),
-                functools.partial(is_high, k),
-            )
-
-        @pl.when(is_low(k))
-        def _():
-            arrived(gram_level.at[k], ("level", k))
-            gram_piece[...] = gram_piece[...] + gram_level[k]
-
-    def gram_sum():
-        arrived(gram_in, ("gram",))
-        total = gram_own[mine, :]
-        for j in range(ROW - 1):
-            total = total + gram_in[j]
-        gram_piece[...] = total
+    gram_sum_z()
+    row_operators(0)
+    for chunk in range(3):
+        send_u(0, chunk)
+
+    def panel_to_row():
+        for j in range(1, ROW):
+            copy(
+                panel.at[mine, :], panel.at[mine, :], ("panel",),
+                base + (r + j) % ROW, lambda: y == 0,
+            )
 
     def panel_out():
-        @pl.when(g == 0)
-        def _():
-            panel[mine, :] = cur2[ROW_CHUNKS[0], :]
-            for j in range(1, ROW):
+        @pl.when(y == 0)
+        def _():
+            panel[mine, :] = cur2[PANEL, :]
+            for j in range(1, YDIM):
                 copy(
-                    cur2.at[ROW_CHUNKS[0], :], panel.at[mine, :],
-                    ("panel",), base + (r + j) % ROW, lambda: g == 0,
+                    panel.at[mine, :], panel.at[mine, :], ("panel y",), y_mate(j),
+                    lambda: y == 0,
                 )
-
-    def gram_out_z():
-        @pl.when(g == 0)
-        def _():
-            arrived(panel.at[pl.ds(0, b - piece), :], ("panel",))
-            square = dot3(panel[mine, :], panel[...], True)
-            gram_all[mine, :] = (gram_piece[...] - square) / float(total_rows)
-            for z in range(1, zdim):
-                copy(
-                    gram_all.at[mine, :], gram_all.at[mine, :], ("gz",),
-                    me + z * YDIM * ROW, lambda: g == 0,
-                )
+            panel_to_row()
+
+    def gather_row(result, chunk, condition):
+        for rank in range(ROW):
+            start = place(3, rank, min(chunk, 1)).start
+            start += eighth_b // 2 if chunk == 2 else 0
+            rows = pl.ds(start, ROW_CHUNKS[chunk].size)
+
+            @pl.when(r == rank)
+            def _():
+                if rank == 0:
+                    gathered[rows, :] = result[ROW_CHUNKS[chunk], :]
+                else:
+                    copy(
+                        result.at[ROW_CHUNKS[chunk], :], gathered.at[rows, :],
+                        ("gather",), base,
+                        functools.partial(lambda o: condition() & (r == o), rank),
+                    )
 
     events = []
     for k in range(row_levels):
@@ -610,14 +749,20 @@
     done = set()
     last = row_levels - 1
     for _, k, chunk in sorted(events):
-        if chunk == 0:
-            row_operators(k)
-        finish_row(k, chunk)
+        if k < last and chunk == 0:
+            forward_operators(k + 1)
+        finish_level(k, chunk)
         if k < last:
-            send_row(k + 1, chunk)
+            if chunk == 0:
+                row_operators(k + 1)
+            send_level(k + 1, chunk)
         done.add((k, chunk))
         if (k, chunk) == (last, 0):
             panel_out()
+        if k == last:
+            @pl.when(g == 0)
+            def _():
+                gather_row(cur2, chunk, lambda: g == 0)
         if (k, chunk) == (0, 2):
             residual(0, gathered)
             residual(1, res1)
@@ -631,73 +776,39 @@
                 @pl.when(r == rank)
                 def _():
                     gather(2, res2, rank, 4, CHUNKS, functools.partial(lambda o: r == o, rank))
-            gram_sum()
-            chain(0)
-            chain(1)
+            gram_sum_x()
         if (k, chunk) == (2, 2):
-            chain(2)
-            if last > 2:
-                chain(3)
-        if last > 3 and (k, chunk) == (4, 0):
-            chain(4)
-        if last > 3 and (k, chunk) == (last - 1, 2):
-            gram_out_z()
-    if last <= 3:
-        gram_out_z()
-
-    def row_result(condition):
-        @pl.when(condition())
+            gram_all_y()
+
+    def row_result(chunk):
+        rows = ROW_CHUNKS[chunk]
+
+        @pl.when(g > 0)
         def _():
             vt = halves(vt_of(slot3))
-            for chunk, rows in enumerate(ROW_CHUNKS):
-                arrived(wbr.at[rows, :], ("wr", chunk))
-                res3[rows, :] = cur2[rows, :] - dot_pairs(halves(wbr[rows, :]), vt)
-                if chunk == 1:
-                    continue
-                for rank in range(ROW):
-                    @pl.when(r == rank)
-                    def _():
-                        gather(
-                            3, res3, rank, 0, (min(chunk, 1),),
-                            functools.partial(lambda o: condition() & (r == o), rank),
-                        )
-
-    half_way = row_count // 2
-    row_result(lambda: (g > 0) & (g != half_way))
-
-    @pl.when(g == 0)
-    def _():
-        for rank in range(ROW):
-            @pl.when(r == rank)
-            def _():
-                gather(
-                    3, cur2, rank, 0, CHUNKS,
-                    functools.partial(lambda o: (g == 0) & (r == o), rank),
-                )
-
-    @pl.when(y == 0)
-    def _():
-        @pl.when(g > 0)
-        def _():
-            arrived(gram_all.at[mine, :], ("gz",))
-
-        for step in range(1, YDIM):
-            copy(
-                gram_all.at[mine, :], gram_all.at[mine, :], ("gy",),
-                me + step * ROW, lambda: y == 0,
-            )
-
-    row_result(lambda: g == half_way)
+            arrived(wbr.at[rows, :], ("wr", chunk))
+            value = wbr[rows, :]
+            if chunk or row_levels < 3:
+                value = value + zr[rows, :]
+                res3[rows, :] = cur2[rows, :] - dot_pairs(halves(value), vt)
+            else:
+                shared = y == 0
+                value = jnp.where(shared, value, value + zr[rows, :])
+                start = jnp.where(shared, res3[rows, :], cur2[rows, :])
+                res3[rows, :] = start - dot_pairs(halves(value), vt)
+            gather_row(res3, chunk, lambda: g > 0)
+
+    for chunk in (1, 2, 0):
+        row_result(chunk)
 
     @pl.when(y != 0)
     def _():
-        arrived(gram_all.at[mine, :], ("gy",))
-
-    for j in range(1, ROW):
-        copy(
-            gram_all.at[mine, :], gram_all.at[mine, :], ("gx",),
-            base + (r + j) % ROW,
-        )
+        arrived(panel.at[mine, :], ("panel y",))
+        for j in range(1, ROW):
+            copy(
+                panel.at[mine, :], panel.at[mine, :], ("panel",),
+                base + (r + j) % ROW, lambda: y != 0,
+            )
 
     @pl.when((r == 2) | (r == 6))
     def _():
@@ -719,8 +830,11 @@
     ]
     for made in local[2:]:
         made.start()
-    arrived(gram_all.at[pl.ds(0, b - piece), :], ("gx",))
-    local.append(pltpu.make_async_copy(gram_all, gram_out, local_sems.at[11]))
+    arrived(gram_all.at[pl.ds(0, b - yrows), :], ("all y",))
+    arrived(panel.at[pl.ds(0, b - piece), :], ("panel",))
+    square = dot3(panel[...], panel[...], True)
+    gram_total[...] = (gram_all[...] - square) / float(total_rows)
+    local.append(pltpu.make_async_copy(gram_total, gram_out, local_sems.at[11]))
     local[-1].start()
 
     for condition, source in pending:
@@ -744,6 +858,7 @@
     total_rows = trailing.shape[0] * devices
     levels = (devices // ROW).bit_length() - 1
     piece = b // ROW
+    zdim = devices // ROW // YDIM
 
     def vmem(*shape, dtype=F32):
         return pltpu.VMEM(shape, dtype)
@@ -758,7 +873,7 @@
         vmem(b // 2 + 8, b),
         *[vmem(b + 8, b)] * 4,
         vmem(3 + levels, b // 2 + 8, b),
-        vmem(b // 2 + 8, b),
+        vmem(b // 2 + 8, b), vmem(b // 2 + 8, b),
         vmem(3 + levels, b, b, dtype=BF16),
         vmem(3 + levels, b, b, dtype=BF16),
         vmem(4, b, b, dtype=BF16),
@@ -772,8 +887,13 @@
         vmem(nc, b),
         vmem(b, nc), vmem(b, nc), vmem(b, b), vmem(b, nc), vmem(b, b),
         vmem(b, 2 * b, dtype=BF16), vmem(b, 2 * b, dtype=BF16),
-        vmem(b, b), vmem(ROW - 1, piece, b), vmem(piece, b), vmem(levels, piece, b),
-        vmem(b, b), vmem(b, b),
+        vmem(b, b),
+        vmem(b // YDIM, b),
+        vmem(YDIM - 1, b // YDIM, b),
+        vmem(max(zdim - 1, 1), b // YDIM // zdim, b),
+        vmem(ROW, b // YDIM // zdim, b),
+        vmem(b, b), vmem(b, b), vmem(b, b),
+        vmem(levels, piece, b),
         pltpu.SemaphoreType.DMA,
         pltpu.SemaphoreType.DMA((RECEIVES,)),
         pltpu.SemaphoreType.DMA((12,)),

time: 74 us -> 67.1 us (0.907)
  the two profiles are of different devices: /device:TPU:129 before, /device:TPU:17 now
where the time goes in v4:
time: 67.1 us; the launch traced here: 66.2 us
  Pallas kernels  60.8 us (91%)
  local copies, waits for them, and re-layouts  4.73 us (7%)
    pallas_call x1, Pallas kernels, body(): pl.pallas_call(functools.partial(tree_kernel, devices, total_rows), out_s...  60.8 us
    unnamed x7, local copies, waits for them, and re-layouts  4.73 us

profile of v4, /device:TPU:17, one launch (start us, length us, event | category | flops | bytes accessed | tf_op | source)
XLA Modules:
  0.0 66.2 jit_solution(1119793831761710867)
XLA Ops:
  0.6 60.8 %tree.1 = (f32[512,1024]{1,0:T(8,128)}, f32[512,256]{1,0:T(8,128)}, f32[256,256]{1,0:T(8,128)}) custom-call(f32[512,1024]{1,0:T(8,128)} %c_hbm.1, f32[512,256]{1,0:T(8,128)} %lv_hbm.1, f32[256,256]{1,0:T(8,128)} %lt_hbm.1, f32[256,256]{1,0:T(8,128)} %tv_hbm.1, f32[256,256]{1,0:T(8,128)} %tt_hbm.1, f32[256,256]{1,0:T(8,128)} %inv_hbm.1), custom_call_target="tpu_custom_call" | custom-call | tf_op jit(solution)/shard_map/tree/pallas_call | solution.py:901
  61.5 0.0 copy-start
  61.5 0.0 copy-start.1
  61.5 3.2 %copy.12 = f32[512,1024]{1,0:T(8,128)} copy(f32[512,1024]{1,0:T(8,128)} %get-tuple-element.6) | data formatting | bytes 4194304
  64.7 0.0 copy-done
  64.7 0.8 %copy.13 = f32[512,256]{1,0:T(8,128)} copy(f32[512,256]{1,0:T(8,128)S(1)} %copy-done) | data formatting | bytes 1048576
  65.5 0.0 copy-done.1
  65.5 0.7 %copy.14 = f32[256,256]{1,0:T(8,128)} copy(f32[256,256]{1,0:T(8,128)S(1)} %copy-done.1) | data formatting | bytes 524288
Async XLA Ops:
  61.5 3.3 %copy-start = (f32[512,256]{1,0:T(8,128)S(1)}, f32[512,256]{1,0:T(8,128)}, u32[]{:S(2)}) copy-start(f32[512,256]{1,0:T(8,128)} %get-tuple-element.7) | copy-start | bytes 1572868
  61.5 4.0 %copy-start.1 = (f32[256,256]{1,0:T(8,128)S(1)}, f32[256,256]{1,0:T(8,128)}, u32[]{:S(2)}) copy-start(f32[256,256]{1,0:T(8,128)} %get-tuple-element.8) | copy-start | bytes 786436

commit v5 on v4

--- a/solution.py
+++ b/solution.py
@@ -38,7 +38,7 @@
     devices,
     total_rows,
     c_hbm, lv_hbm, lt_hbm, tv_hbm, tt_hbm, inv_hbm,
-    upd_out, basis_out, gram_out,
+    head_rows, rest, head_basis, rest_basis, gram_total,
     c_ref, lv_ref, lt_ref, tv_ref, tt_ref, inv_ref,
     pack,
     folded,
@@ -53,9 +53,9 @@
     zr, inr, wr, wbr,
     res1, res2, res3,
     gathered,
-    coef, rest, rest_basis, head_rows, head_basis,
+    coef,
     lvt_high, lvt_low,
-    gram_own, gram_piece, gram_y, gram_z, gram_x, panel, gram_all, gram_total, wback,
+    gram_own, gram_piece, gram_y, gram_z, gram_x, panel, gram_all, wback,
     send_sem, recv_sems, local_sems,
 ):
     b = pack.shape[1]
@@ -472,10 +472,6 @@
     finish(0, 1)
     send(1, 1)
 
-    @pl.when((r == 0) & (g > 0))
-    def _():
-        copy(pack, slot3, ("slot", 3), base + 4, lambda: (r == 0) & (g > 0))
-
     @pl.when((r == 0) | (r == 4))
     def _():
         arrived(folds[1], ("fold", 1))
@@ -485,6 +481,15 @@
     give_back(0, 0)
     give_back(0, 1)
     gram_start()
+
+    @pl.when(((r == 2) | (r == 6)) & (g > 0))
+    def _():
+        arrived(slot3, ("slot", 3))
+        copy(slot3, slot3, ("slot", 3), me + 1, lambda: ((r == 2) | (r == 6)) & (g > 0))
+
+        @pl.when(r == 2)
+        def _():
+            copy(slot3, slot3, ("slot", 3), me + 2, lambda: (r == 2) & (g > 0))
 
     @pl.when(r == 6)
     def _():
@@ -518,13 +523,10 @@
 
     @pl.when((g > 0) & (core == 0))
     def _():
-        @pl.when(r > 0)
+        @pl.when(r == 4)
         def _():
             arrived(slot3, ("slot", 3))
-            copy(
-                slot3, slot3, ("slot", 3), me + 1,
-                lambda: (g > 0) & (core == 0) & (r > 0),
-            )
+            copy(slot3, slot3, ("slot", 3), me + 1, lambda: (g > 0) & (r == 4))
 
         make_fold(row_fold, t_of(slot3))
 
@@ -565,12 +567,6 @@
     rest_basis[...] = dot3(rest[:, :b], inv_ref[...])
     for tile in range(1, nc // b):
         rest_tile(tile)
-    local = [
-        pltpu.make_async_copy(rest, upd_out.at[pl.ds(b, b), :], local_sems.at[7]),
-        pltpu.make_async_copy(rest_basis, basis_out.at[pl.ds(b, b), :], local_sems.at[8]),
-    ]
-    for made in local:
-        made.start()
 
     @pl.when((g > 0) & (core == 1))
     def _():
@@ -703,7 +699,6 @@
     give_back(2, 0)
     give_back(2, 1)
 
-    gram_sum_z()
     row_operators(0)
     for chunk in range(3):
         send_u(0, chunk)
@@ -745,7 +740,8 @@
 
     events = []
     for k in range(row_levels):
-        events += [(2.9 * k, k, 0), (2.0 + 4.2 * k, k, 1), (2.9 + 4.2 * k, k, 2)]
+        events += [(2.9 * k + (5.0 if k > 3 else 0.0), k, 0)]
+        events += [(2.0 + 4.2 * k, k, 1), (2.9 + 4.2 * k, k, 2)]
     done = set()
     last = row_levels - 1
     for _, k, chunk in sorted(events):
@@ -764,6 +760,7 @@
             def _():
                 gather_row(cur2, chunk, lambda: g == 0)
         if (k, chunk) == (0, 2):
+            gram_sum_z()
             residual(0, gathered)
             residual(1, res1)
             for rank, into in ((2, 2), (3, 2), (6, 6), (7, 6)):
@@ -777,7 +774,7 @@
                 def _():
                     gather(2, res2, rank, 4, CHUNKS, functools.partial(lambda o: r == o, rank))
             gram_sum_x()
-        if (k, chunk) == (2, 2):
+        if (k, chunk) == (min(last, 3), 2):
             gram_all_y()
 
     def row_result(chunk):
@@ -824,18 +821,10 @@
 
     head_rows[...] = gathered[...].T
     head_basis[...] = jnp.where(me == 0, 0.0, dot3(head_rows[:, :b], inv_ref[...]))
-    local += [
-        pltpu.make_async_copy(head_rows, upd_out.at[pl.ds(0, b), :], local_sems.at[9]),
-        pltpu.make_async_copy(head_basis, basis_out.at[pl.ds(0, b), :], local_sems.at[10]),
-    ]
-    for made in local[2:]:
-        made.start()
     arrived(gram_all.at[pl.ds(0, b - yrows), :], ("all y",))
     arrived(panel.at[pl.ds(0, b - piece), :], ("panel",))
     square = dot3(panel[...], panel[...], True)
     gram_total[...] = (gram_all[...] - square) / float(total_rows)
-    local.append(pltpu.make_async_copy(gram_total, gram_out, local_sems.at[11]))
-    local[-1].start()
 
     for condition, source in pending:
         made = functools.partial(
@@ -847,9 +836,27 @@
             @pl.when(condition())
             def _():
                 made()
-    for made in local:
+    assert len(numbers) <= recv_sems.shape[0]
+
+
+def write_kernel(
+    head_rows, rest, head_basis, rest_basis, gram, upd_out, basis_out, gram_out, sems
+):
+    b = head_rows.shape[0]
+    copies = [
+        pltpu.make_async_copy(source, target, sems.at[index])
+        for index, (source, target) in enumerate((
+            (head_rows, upd_out.at[pl.ds(0, b), :]),
+            (rest, upd_out.at[pl.ds(b, b), :]),
+            (head_basis, basis_out.at[pl.ds(0, b), :]),
+            (rest_basis, basis_out.at[pl.ds(b, b), :]),
+            (gram, gram_out),
+        ))
+    ]
+    for made in copies:
+        made.start()
+    for made in copies:
         made.wait()
-    assert len(numbers) <= recv_sems.shape[0]
 
 
 def body(trailing, leaf_vectors, leaf_factors, tree_vectors, tree_factors, inverse_factor):
@@ -885,28 +892,26 @@
         vmem(nc // 8, b),
         *per_level,
         vmem(nc, b),
-        vmem(b, nc), vmem(b, nc), vmem(b, b), vmem(b, nc), vmem(b, b),
+        vmem(b, nc),
         vmem(b, 2 * b, dtype=BF16), vmem(b, 2 * b, dtype=BF16),
         vmem(b, b),
         vmem(b // YDIM, b),
         vmem(YDIM - 1, b // YDIM, b),
         vmem(max(zdim - 1, 1), b // YDIM // zdim, b),
         vmem(ROW, b // YDIM // zdim, b),
-        vmem(b, b), vmem(b, b), vmem(b, b),
+        vmem(b, b), vmem(b, b),
         vmem(levels, piece, b),
         pltpu.SemaphoreType.DMA,
         pltpu.SemaphoreType.DMA((RECEIVES,)),
-        pltpu.SemaphoreType.DMA((12,)),
+        pltpu.SemaphoreType.DMA((7,)),
     ]
-    return pl.pallas_call(
+    results = pl.pallas_call(
         functools.partial(tree_kernel, devices, total_rows),
         out_shape=(
-            jax.ShapeDtypeStruct(trailing.shape, F32),
-            jax.ShapeDtypeStruct(leaf_vectors.shape, F32),
-            jax.ShapeDtypeStruct((b, b), F32),
+            vmem(b, nc), vmem(b, nc), vmem(b, b), vmem(b, b), vmem(b, b)
         ),
-        in_specs=[pl.BlockSpec(memory_space=pl.ANY)] * 6,
-        out_specs=[pl.BlockSpec(memory_space=pl.ANY)] * 3,
+        in_specs=[pl.BlockSpec(memory_space=pltpu.HBM)] * 6,
+        out_specs=[pl.BlockSpec(memory_space=pltpu.VMEM)] * 5,
         scratch_shapes=scratch,
         compiler_params=pltpu.CompilerParams(
             collective_id=0,
@@ -915,6 +920,18 @@
         ),
         name="tree",
     )(*arguments)
+    return pl.pallas_call(
+        write_kernel,
+        out_shape=(
+            jax.ShapeDtypeStruct(trailing.shape, F32),
+            jax.ShapeDtypeStruct(leaf_vectors.shape, F32),
+            jax.ShapeDtypeStruct((b, b), F32),
+        ),
+        in_specs=[pl.BlockSpec(memory_space=pltpu.VMEM)] * 5,
+        out_specs=[pl.BlockSpec(memory_space=pl.ANY)] * 3,
+        scratch_shapes=[pltpu.SemaphoreType.DMA((5,))],
+        name="write",
+    )(*[pltpu.with_memory_space_constraint(result, pltpu.VMEM) for result in results])
 
 
 def solution(mesh):

time: 67.1 us -> 63.1 us (0.940)
  local copies, waits for them, and re-layouts: 4.73 us -> 0 us
    unnamed x7 -> x0, local copies, waits for them, and re-layouts: 4.73 us -> none
    pallas_call x0 -> x1, Pallas kernels: none -> 1.61 us  [body(): pl.pallas_call(write_kernel, out_shape=(jax.ShapeDtypeStruct(trailing.sha...]
    pallas_call x1, Pallas kernels: 60.8 us -> 59.8 us  [body(): pl.pallas_call(functools.partial(tree_kernel, devices, total_rows), out_s...]
where the time goes in v5:
time: 63.1 us; the launch traced here: 62.2 us
  Pallas kernels  61.4 us (97%)
  between operations  0.8 us (1%)
    pallas_call x1, Pallas kernels, body(): pl.pallas_call(functools.partial(tree_kernel, devices, total_rows), out_s...  59.8 us
    pallas_call x1, Pallas kernels, body(): pl.pallas_call(write_kernel, out_shape=(jax.ShapeDtypeStruct(trailing.sha...  1.61 us

profile of v5, /device:TPU:17, one launch (start us, length us, event | category | flops | bytes accessed | tf_op | source)
XLA Modules:
  0.0 62.2 jit_solution(4079655929939239597)
XLA Ops:
  0.6 59.8 %tree.1 = (f32[256,1024]{1,0:T(8,128)S(1)}, f32[256,1024]{1,0:T(8,128)S(1)}, f32[256,256]{1,0:T(8,128)S(1)}, f32[256,256]{1,0:T(8,128)S(1)}, f32[256,256]{1,0:T(8,128)S(1)}) custom-call(f32[512,1024]{1,0:T(8,128)} %c_hbm.1, f32[512,256]{1,0:T(8,128)} %lv_hbm.1, f32[256,256]{1,0:T(8,128)} %lt_hbm.1, f32[256,256]{1,0:T(8,128)} %tv_hbm.1, f32[256,256]{1,0:T(8,128)} %tt_hbm.1, ...), custom_call_target="tpu_custom_call" | custom-call | tf_op jit(solution)/shard_map/tree/pallas_call | solution.py:908
  60.4 1.6 %write.1 = (f32[512,1024]{1,0:T(8,128)}, f32[512,256]{1,0:T(8,128)}, f32[256,256]{1,0:T(8,128)}) custom-call(f32[256,1024]{1,0:T(8,128)S(1)} %get-tuple-element.8.head_rows, f32[256,1024]{1,0:T(8,128)S(1)} %get-tuple-element.9.rest, f32[256,256]{1,0:T(8,128)S(1)} %get-tuple-element.10.head_basis, f32[256,256]{1,0:T(8,128)S(1)} %get-tuple-element.11.rest_basis, ...), custom_call_target="tpu_custom_call" | custom-call | tf_op jit(solution)/shard_map/write/pallas_call | solution.py:923

commit v6 on v5

--- a/solution.py
+++ b/solution.py
@@ -75,6 +75,7 @@
     base = g * ROW
     y = g % YDIM
     z = g // YDIM
+    twin = base + r + 1 - 2 * core
     neighbour = base + (r + 1) % ROW
 
     def y_mate(j):
@@ -468,7 +469,6 @@
         t_from_slot(1)
 
     send(1, 0)
-
     finish(0, 1)
     send(1, 1)
 
@@ -611,47 +611,58 @@
     PANEL = ROW_CHUNKS[0]
 
     def send_shared(k):
-        ours = wr.at[k, PANEL, :]
+        ours, ahead = wr.at[k, PANEL, :], backs[k]
 
         @pl.when(low_half(k))
         def _():
             value = cur2[PANEL, :]
-            wr[k, PANEL, :] = value - times_t(value, 3 + k)
-            copy(
-                ours, inr.at[k, PANEL, :], ("z", k, 0), me + (ROW << k),
-                functools.partial(low_half, k),
-            )
+            update = times_t(value, 3 + k)
+            wr[k, PANEL, :] = value - update
+            if k != 4:
+                copy(
+                    ours, inr.at[k, PANEL, :], ("z", k, 0), me + (ROW << k),
+                    functools.partial(low_half, k),
+                )
+
+            @pl.when(is_low(k))
+            def _():
+                wback[k, :, :] = update
+                copy(
+                    ahead, wbr.at[PANEL, :], ("wr", 0), me + (ROW << k),
+                    functools.partial(is_low, k),
+                )
 
         @pl.when(high_half(k))
         def _():
-            wr[k, PANEL, :] = -times_t(cur2[PANEL, :], 3 + k)
-            copy(
-                ours, inr.at[k, PANEL, :], ("z", k, 0), me - (ROW << k),
-                functools.partial(high_half, k),
-            )
+            update = times_t(cur2[PANEL, :], 3 + k)
+            wr[k, PANEL, :] = -update
+
+            @pl.when(is_high(k))
+            def _():
+                zr[PANEL, :] = update
+                res3[PANEL, :] = cur2[PANEL, :]
+
+            if k != 4:
+                copy(
+                    ours, inr.at[k, PANEL, :], ("z", k, 0), me - (ROW << k),
+                    functools.partial(high_half, k),
+                )
+
+        if k == 4:
+            for source, targets in ((7, (1, 0)), (4, (2, 3)), (3, (5, 4)), (0, (6, 7))):
+                @pl.when((y == 0) & (z == source))
+                def _():
+                    for target in targets:
+                        copy(
+                            ours, inr.at[k, PANEL, :], ("z", k, 0),
+                            target * YDIM * ROW + r,
+                            functools.partial(lambda o: (y == 0) & (z == o), source),
+                        )
 
     def finish_shared(k):
-        back = backs[k]
-
         @pl.when(y == 0)
         def _():
             arrived(inr.at[k, PANEL, :], ("z", k, 0))
-
-        @pl.when(is_high(k))
-        def _():
-            res3[PANEL, :] = cur2[PANEL, :]
-
-        @pl.when(is_low(k))
-        def _():
-            value = cur2[PANEL, :] - (wr[k, PANEL, :] + inr[k, PANEL, :])
-            wback[k, :, :] = value
-            copy(
-                back, wbr.at[PANEL, :], ("wr", 0), me + (ROW << k),
-                functools.partial(is_low, k),
-            )
-
-        @pl.when(y == 0)
-        def _():
             cur2[PANEL, :] = wr[k, PANEL, :] + inr[k, PANEL, :]
 
     def send_level(k, chunk):
@@ -703,11 +714,12 @@
     for chunk in range(3):
         send_u(0, chunk)
 
-    def panel_to_row():
-        for j in range(1, ROW):
+    def panel_to_row(condition):
+        copy(panel.at[mine, :], panel.at[mine, :], ("panel core",), twin, condition)
+        for j in (4, 2, 6):
             copy(
                 panel.at[mine, :], panel.at[mine, :], ("panel",),
-                base + (r + j) % ROW, lambda: y == 0,
+                base + (r + j) % ROW, condition,
             )
 
     def panel_out():
@@ -719,7 +731,7 @@
                     panel.at[mine, :], panel.at[mine, :], ("panel y",), y_mate(j),
                     lambda: y == 0,
                 )
-            panel_to_row()
+            panel_to_row(lambda: y == 0)
 
     def gather_row(result, chunk, condition):
         for rank in range(ROW):
@@ -737,6 +749,20 @@
                         ("gather",), base,
                         functools.partial(lambda o: condition() & (r == o), rank),
                     )
+
+    def row_result(k):
+        for chunk in (1, 2, 0):
+            rows = ROW_CHUNKS[chunk]
+
+            @pl.when(is_high(k))
+            def _():
+                vt = halves(vt_of(slot3))
+                arrived(wbr.at[rows, :], ("wr", chunk))
+                start = res3 if k > 1 and chunk == 0 else cur2
+                res3[rows, :] = start[rows, :] - dot_pairs(
+                    halves(wbr[rows, :] + zr[rows, :]), vt
+                )
+                gather_row(res3, chunk, functools.partial(is_high, k))
 
     events = []
     for k in range(row_levels):
@@ -755,6 +781,8 @@
         done.add((k, chunk))
         if (k, chunk) == (last, 0):
             panel_out()
+        if (k, chunk) == (last, 0 if last > 3 else 2):
+            gram_all_y()
         if k == last:
             @pl.when(g == 0)
             def _():
@@ -774,38 +802,20 @@
                 def _():
                     gather(2, res2, rank, 4, CHUNKS, functools.partial(lambda o: r == o, rank))
             gram_sum_x()
-        if (k, chunk) == (min(last, 3), 2):
-            gram_all_y()
-
-    def row_result(chunk):
-        rows = ROW_CHUNKS[chunk]
-
-        @pl.when(g > 0)
-        def _():
-            vt = halves(vt_of(slot3))
-            arrived(wbr.at[rows, :], ("wr", chunk))
-            value = wbr[rows, :]
-            if chunk or row_levels < 3:
-                value = value + zr[rows, :]
-                res3[rows, :] = cur2[rows, :] - dot_pairs(halves(value), vt)
-            else:
-                shared = y == 0
-                value = jnp.where(shared, value, value + zr[rows, :])
-                start = jnp.where(shared, res3[rows, :], cur2[rows, :])
-                res3[rows, :] = start - dot_pairs(halves(value), vt)
-            gather_row(res3, chunk, lambda: g > 0)
-
-    for chunk in (1, 2, 0):
-        row_result(chunk)
+        if k and chunk == 2:
+            row_result(k - 1)
+        if (k, chunk) == (last, 2):
+            row_result(last)
 
     @pl.when(y != 0)
     def _():
         arrived(panel.at[mine, :], ("panel y",))
-        for j in range(1, ROW):
-            copy(
-                panel.at[mine, :], panel.at[mine, :], ("panel",),
-                base + (r + j) % ROW, lambda: y != 0,
-            )
+        panel_to_row(lambda: y != 0)
+
+    arrived(panel.at[pl.ds(0, 3 * piece), :], ("panel",))
+    for j in (2, 6, 4):
+        theirs = piece_of((r + j) % ROW)
+        copy(panel.at[theirs, :], panel.at[theirs, :], ("panel core",), twin)
 
     @pl.when((r == 2) | (r == 6))
     def _():
@@ -822,7 +832,7 @@
     head_rows[...] = gathered[...].T
     head_basis[...] = jnp.where(me == 0, 0.0, dot3(head_rows[:, :b], inv_ref[...]))
     arrived(gram_all.at[pl.ds(0, b - yrows), :], ("all y",))
-    arrived(panel.at[pl.ds(0, b - piece), :], ("panel",))
+    arrived(panel.at[pl.ds(0, 4 * piece), :], ("panel core",))
     square = dot3(panel[...], panel[...], True)
     gram_total[...] = (gram_all[...] - square) / float(total_rows)
 

time: 63.1 us -> 60.7 us (0.962); the launches traced: 62.2 us -> 60.6 us
  Pallas kernels: 61.4 us -> 59.8 us
    pallas_call x1, Pallas kernels: 59.8 us -> 58.2 us  [body(): pl.pallas_call(functools.partial(tree_kernel, devices, total_rows), out_s...]
where the time goes in v6:
time: 60.7 us; the launch traced here: 60.6 us
  Pallas kernels  59.8 us (99%)
  between operations  0.8 us (1%)
    pallas_call x1, Pallas kernels, body(): pl.pallas_call(functools.partial(tree_kernel, devices, total_rows), out_s...  58.2 us
    pallas_call x1, Pallas kernels, body(): pl.pallas_call(write_kernel, out_shape=(jax.ShapeDtypeStruct(trailing.sha...  1.61 us

profile of v6, /device:TPU:17, one launch (start us, length us, event | category | flops | bytes accessed | tf_op | source)
XLA Modules:
  0.0 60.6 jit_solution(8475406071022555313)
XLA Ops:
  0.6 58.2 %tree.1 = (f32[256,1024]{1,0:T(8,128)S(1)}, f32[256,1024]{1,0:T(8,128)S(1)}, f32[256,256]{1,0:T(8,128)S(1)}, f32[256,256]{1,0:T(8,128)S(1)}, f32[256,256]{1,0:T(8,128)S(1)}) custom-call(f32[512,1024]{1,0:T(8,128)} %c_hbm.1, f32[512,256]{1,0:T(8,128)} %lv_hbm.1, f32[256,256]{1,0:T(8,128)} %lt_hbm.1, f32[256,256]{1,0:T(8,128)} %tv_hbm.1, f32[256,256]{1,0:T(8,128)} %tt_hbm.1, ...), custom_call_target="tpu_custom_call" | custom-call | tf_op jit(solution)/shard_map/tree/pallas_call | solution.py:918
  58.8 1.6 %write.1 = (f32[512,1024]{1,0:T(8,128)}, f32[512,256]{1,0:T(8,128)}, f32[256,256]{1,0:T(8,128)}) custom-call(f32[256,1024]{1,0:T(8,128)S(1)} %get-tuple-element.8.head_rows, f32[256,1024]{1,0:T(8,128)S(1)} %get-tuple-element.9.rest, f32[256,256]{1,0:T(8,128)S(1)} %get-tuple-element.10.head_basis, f32[256,256]{1,0:T(8,128)S(1)} %get-tuple-element.11.rest_basis, ...), custom_call_target="tpu_custom_call" | custom-call | tf_op jit(solution)/shard_map/write/pallas_call | solution.py:933

commit v7 on v6

--- a/solution.py
+++ b/solution.py
@@ -139,13 +139,14 @@
         ("tv", tv_hbm, tv_ref),
         ("tt", tt_hbm, tt_ref),
         ("lv", lv_hbm, lv_ref),
+        ("lt", lt_hbm, lt_ref),
         ("c0", c_hbm.at[:, pl.ds(0, b)], c_ref.at[:, pl.ds(0, b)]),
-        ("lt", lt_hbm, lt_ref),
         ("c1", c_hbm.at[:, pl.ds(b, nc - b)], c_ref.at[:, pl.ds(b, nc - b)]),
         ("inv", inv_hbm, inv_ref),
     ):
         loads[name] = pltpu.make_async_copy(source, target, local_sems.at[len(loads)])
-        loads[name].start()
+        if name not in ("c1", "inv"):
+            loads[name].start()
 
     barrier = pltpu.get_barrier_semaphore()
 
@@ -246,15 +247,18 @@
     pack[b:, :] = jnp.broadcast_to(diagonal, (8, b))
     make_fold(folded, tt)
 
+    def own_node(index):
+        slot[index][...] = pack[...]
+        make_bt(index)
+        if index < 3:
+            t_from_slot(index)
+
     for condition, index in (
         (core == 1, 0), ((r == 2) | (r == 6), 1), (r == 4, 2), ((r == 0) & (g > 0), 3),
     ):
         @pl.when(condition)
         def _():
-            slot[index][...] = pack[...]
-            make_bt(index)
-            if index < 3:
-                t_from_slot(index)
+            own_node(index)
 
     loads["lv"].wait()
     high, low = halves(lv_ref[...].T)
@@ -269,8 +273,10 @@
         result = c_ref[:b, columns] - dot3(lv_ref[:b, :], coeffs)
         head[columns, :] = result.T
 
+    loads["lt"].wait()
     loads["c0"].wait()
-    loads["lt"].wait()
+    loads["c1"].start()
+    loads["inv"].start()
     leaf_tile(0)
     entered()
 
@@ -286,7 +292,6 @@
 
     @pl.when(r == 4)
     def _():
-        copy(folded, folds[2], ("fold", 2), base, lambda: r == 4)
         copy(pack, slot2, ("slot", 2), base + 5, lambda: r == 4)
         copy(folded, folds[2], ("fold", 2), base + 2, lambda: r == 4)
         copy(pack, slot2, ("slot", 2), base + 6, lambda: r == 4)
@@ -482,6 +487,13 @@
     give_back(0, 1)
     gram_start()
 
+    @pl.when(r == 2)
+    def _():
+        arrived(folds[2], ("fold", 2))
+        copy(folds[2], folds[2], ("fold", 2), me - 2, lambda: r == 2)
+        copy(folds[2], folds[2], ("fold", 2), me + 1, lambda: r == 2)
+        t_from_fold(2)
+
     @pl.when(((r == 2) | (r == 6)) & (g > 0))
     def _():
         arrived(slot3, ("slot", 3))
@@ -512,14 +524,15 @@
     finish(1, 0)
     send(2, 0)
 
-    @pl.when((r == 0) | (r == 2))
-    def _():
-        arrived(folds[2], ("fold", 2))
-        copy(folds[2], folds[2], ("fold", 2), me + 1, lambda: (r == 0) | (r == 2))
-        t_from_fold(2)
-
     finish(1, 1)
     send(2, 1)
+
+    @pl.when(r == 0)
+    def _():
+        arrived(folds[2], ("fold", 2))
+        copy(folds[2], folds[2], ("fold", 2), me + 1, lambda: r == 0)
+        t_from_fold(2)
+
 
     @pl.when((g > 0) & (core == 0))
     def _():

time: 60.7 us -> 58.9 us (0.970)
  Pallas kernels: 59.8 us -> 57.8 us
    pallas_call x1, Pallas kernels: 58.2 us -> 56.2 us  [body(): pl.pallas_call(functools.partial(tree_kernel, devices, total_rows), out_s...]
where the time goes in v7:
time: 58.9 us; the launch traced here: 58.6 us
  Pallas kernels  57.8 us (98%)
  between operations  0.8 us (1%)
    pallas_call x1, Pallas kernels, body(): pl.pallas_call(functools.partial(tree_kernel, devices, total_rows), out_s...  56.2 us
    pallas_call x1, Pallas kernels, body(): pl.pallas_call(write_kernel, out_shape=(jax.ShapeDtypeStruct(trailing.sha...  1.61 us

profile of v7, /device:TPU:17, one launch (start us, length us, event | category | flops | bytes accessed | tf_op | source)
XLA Modules:
  0.0 58.6 jit_solution(17876508279926344012)
XLA Ops:
  0.6 56.2 %tree.1 = (f32[256,1024]{1,0:T(8,128)S(1)}, f32[256,1024]{1,0:T(8,128)S(1)}, f32[256,256]{1,0:T(8,128)S(1)}, f32[256,256]{1,0:T(8,128)S(1)}, f32[256,256]{1,0:T(8,128)S(1)}) custom-call(f32[512,1024]{1,0:T(8,128)} %c_hbm.1, f32[512,256]{1,0:T(8,128)} %lv_hbm.1, f32[256,256]{1,0:T(8,128)} %lt_hbm.1, f32[256,256]{1,0:T(8,128)} %tv_hbm.1, f32[256,256]{1,0:T(8,128)} %tt_hbm.1, ...), custom_call_target="tpu_custom_call" | custom-call | tf_op jit(solution)/shard_map/tree/pallas_call | solution.py:931
  56.8 1.6 %write.1 = (f32[512,1024]{1,0:T(8,128)}, f32[512,256]{1,0:T(8,128)}, f32[256,256]{1,0:T(8,128)}) custom-call(f32[256,1024]{1,0:T(8,128)S(1)} %get-tuple-element.8.head_rows, f32[256,1024]{1,0:T(8,128)S(1)} %get-tuple-element.9.rest, f32[256,256]{1,0:T(8,128)S(1)} %get-tuple-element.10.head_basis, f32[256,256]{1,0:T(8,128)S(1)} %get-tuple-element.11.rest_basis, ...), custom_call_target="tpu_custom_call" | custom-call | tf_op jit(solution)/shard_map/write/pallas_call | solution.py:946

commit v8 on v7

--- a/solution.py
+++ b/solution.py
@@ -503,6 +503,32 @@
         def _():
             copy(slot3, slot3, ("slot", 3), me + 2, lambda: (r == 2) & (g > 0))
 
+    def row_node(condition):
+        @pl.when(condition())
+        def _():
+            make_fold(row_fold, t_of(slot3))
+
+            @pl.when(r > 0)
+            def _():
+                make_bt(3)
+
+            if row_levels > 2:
+                make_fold(row_fold_bt, bt_high[3].astype(F32) + bt_low[3].astype(F32))
+            for k in range(row_levels):
+                @pl.when(is_high(k))
+                def _():
+                    c = functools.partial(lambda k: is_high(k) & condition(), k)
+                    name = ("fold", 3 + k)
+                    for j in range(max(1, (1 << k) // YDIM)):
+                        copy(
+                            row_fold, folds[3 + k], name,
+                            me - (ROW << k) + j * YDIM * ROW, c,
+                        )
+                        if j:
+                            copy(row_fold_bt, folds[3 + k], name, me + j * YDIM * ROW, c)
+
+    row_node(lambda: (g > 0) & (core == 0) & (r != 4))
+
     @pl.when(r == 6)
     def _():
         arrived(slot2, ("slot", 2))
@@ -534,33 +560,12 @@
         t_from_fold(2)
 
 
-    @pl.when((g > 0) & (core == 0))
-    def _():
-        @pl.when(r == 4)
-        def _():
-            arrived(slot3, ("slot", 3))
-            copy(slot3, slot3, ("slot", 3), me + 1, lambda: (g > 0) & (r == 4))
-
-        make_fold(row_fold, t_of(slot3))
-
-        @pl.when(r > 0)
-        def _():
-            make_bt(3)
-
-        if row_levels > 2:
-            make_fold(row_fold_bt, bt_high[3].astype(F32) + bt_low[3].astype(F32))
-        for k in range(row_levels):
-            @pl.when(is_high(k))
-            def _():
-                c = functools.partial(lambda k: is_high(k) & (core == 0), k)
-                name = ("fold", 3 + k)
-                for j in range(max(1, (1 << k) // YDIM)):
-                    copy(
-                        row_fold, folds[3 + k], name,
-                        me - (ROW << k) + j * YDIM * ROW, c,
-                    )
-                    if j:
-                        copy(row_fold_bt, folds[3 + k], name, me + j * YDIM * ROW, c)
+    @pl.when((g > 0) & (r == 4))
+    def _():
+        arrived(slot3, ("slot", 3))
+        copy(slot3, slot3, ("slot", 3), me + 1, lambda: (g > 0) & (r == 4))
+
+    row_node(lambda: (g > 0) & (r == 4))
 
     give_back(1, 0)
     give_back(1, 1)
@@ -786,10 +791,9 @@
     for _, k, chunk in sorted(events):
         if k < last and chunk == 0:
             forward_operators(k + 1)
+            row_operators(k + 1)
         finish_level(k, chunk)
         if k < last:
-            if chunk == 0:
-                row_operators(k + 1)
             send_level(k + 1, chunk)
         done.add((k, chunk))
         if (k, chunk) == (last, 0):

time: 58.9 us -> 58.2 us (0.988)
  Pallas kernels: 57.8 us -> 57.2 us
where the time goes in v8:
time: 58.2 us; the launch traced here: 58 us
  Pallas kernels  57.2 us (98%)
  between operations  0.8 us (1%)
    pallas_call x1, Pallas kernels, body(): pl.pallas_call(functools.partial(tree_kernel, devices, total_rows), out_s...  55.6 us
    pallas_call x1, Pallas kernels, body(): pl.pallas_call(write_kernel, out_shape=(jax.ShapeDtypeStruct(trailing.sha...  1.61 us

profile of v8, /device:TPU:17, one launch (start us, length us, event | category | flops | bytes accessed | tf_op | source)
XLA Modules:
  0.0 58.0 jit_solution(17727098759971079619)
XLA Ops:
  0.6 55.6 %tree.1 = (f32[256,1024]{1,0:T(8,128)S(1)}, f32[256,1024]{1,0:T(8,128)S(1)}, f32[256,256]{1,0:T(8,128)S(1)}, f32[256,256]{1,0:T(8,128)S(1)}, f32[256,256]{1,0:T(8,128)S(1)}) custom-call(f32[512,1024]{1,0:T(8,128)} %c_hbm.1, f32[512,256]{1,0:T(8,128)} %lv_hbm.1, f32[256,256]{1,0:T(8,128)} %lt_hbm.1, f32[256,256]{1,0:T(8,128)} %tv_hbm.1, f32[256,256]{1,0:T(8,128)} %tt_hbm.1, ...), custom_call_target="tpu_custom_call" | custom-call | tf_op jit(solution)/shard_map/tree/pallas_call | solution.py:935
  56.3 1.6 %write.1 = (f32[512,1024]{1,0:T(8,128)}, f32[512,256]{1,0:T(8,128)}, f32[256,256]{1,0:T(8,128)}) custom-call(f32[256,1024]{1,0:T(8,128)S(1)} %get-tuple-element.8.head_rows, f32[256,1024]{1,0:T(8,128)S(1)} %get-tuple-element.9.rest, f32[256,256]{1,0:T(8,128)S(1)} %get-tuple-element.10.head_basis, f32[256,256]{1,0:T(8,128)S(1)} %get-tuple-element.11.rest_basis, ...), custom_call_target="tpu_custom_call" | custom-call | tf_op jit(solution)/shard_map/write/pallas_call | solution.py:950
